TPU v7x, 1024 devices: a whole 8x8x8 slice. The times are simulated.
1024 devices in a mesh: gx: 16 (over z, x_hi), gy: 8 (over x_lo, core), gz: 8 (over y).
Axes of the slice: x: 8 (x_hi: 2, x_lo: 4; x = x_hi * 4 + x_lo), y: 8, z: 8, core: 2. Of those that a mesh axis runs over, the one named last changes fastest.
Arguments:
- terminal_adjoint: float32 [5, 128, 64, 1024], P(None, 'gx', 'gy', 'gz'), may hold values from -6 to 6
- density: float32 [128, 64, 1024], P('gx', 'gy', 'gz'), may hold values from 0.7 to 1.5
- velocity: float32 [3, 128, 64, 1024], P(None, 'gx', 'gy', 'gz'), may hold values from -0.5 to 0.5
- stiffness: float32 [128, 64, 1024], P('gx', 'gy', 'gz'), may hold values from 0.6 to 1.6
- sponge: float32 [128, 64, 1024], P('gx', 'gy', 'gz'), may hold values from 0.1 to 3
- source_shape: float32 [128, 64, 1024], P('gx', 'gy', 'gz'), may hold values from -0.1875 to 0.1875
- brick_level: int32 [16, 8, 8], replicated, may hold values from 0 to 1
- brick_patch: int32 [16, 8, 8], replicated, may hold values from 0 to 1023, as said below
- patch_owner: int32 [1024], replicated, may hold values from 0 to 1023, as said below
Outputs:
- adjoint: float32 [5, 128, 64, 1024], P(None, 'gx', 'gy', 'gz')
- patch_gradient: float32 [1024, 40], P(('gx', 'gy', 'gz'))
Inputs may be any that keep to these rules, and one draw needn't show every extreme that they name: `brick_patch`: each brick names one patch; a patch may be named by several bricks or by none. `patch_owner`: every device owns exactly one patch.
All inputs are finite; a program needn't handle non-finite values.
Results may differ from a plain program's by a relative error of at most 0.00013.
Values sent between devices are 32-bit elements; how exact they have to be, the bound alone decides.
A program may use at most 32 MiB of HBM per device.

v0:
```python
import jax
import jax.numpy as jnp
from jax import lax
from jax.sharding import PartitionSpec as P

BX = 8
BY = 8
BZ = 16


step_length = 0.14
third = 1.0 / 3.0
two_thirds = 2.0 / 3.0


def with_halo(block, sides, width):
    for axis, dim in sides:
        count = lax.axis_size(axis)
        forward = [(i, i + 1) for i in range(count - 1)]
        backward = [(target, source) for source, target in forward]
        low = lax.ppermute(
            lax.slice_in_dim(block, block.shape[dim] - width, None, axis=dim), axis, forward
        )
        high = lax.ppermute(lax.slice_in_dim(block, 0, width, axis=dim), axis, backward)
        block = jnp.concatenate([low, block, high], axis=dim)
    return block


def transposed_flux(adjoint, density, velocity, stiffness, direction):
    along_speed = velocity[direction]
    components = [along_speed * adjoint[component] for component in range(5)]
    velocity_row = 1 + direction
    components[velocity_row] = (
        components[velocity_row] + density * adjoint[0] + stiffness * adjoint[4]
    )
    components[4] = components[4] + adjoint[velocity_row] / density
    return jnp.stack(components)


def apply_faces(adjoint, density, velocity, stiffness, half_inverse, sponge):
    partials = half_inverse * transposed_flux(adjoint, density, velocity, stiffness, 0)
    padded = with_halo(partials, (("gx", 1),), 1)
    summed = padded[:, 2:] - padded[:, :-2]
    partials = half_inverse * transposed_flux(adjoint, density, velocity, stiffness, 1)
    padded = with_halo(partials, (("gy", 2),), 1)
    summed = summed + (padded[:, :, 2:] - padded[:, :, :-2])
    partials = half_inverse * transposed_flux(adjoint, density, velocity, stiffness, 2)
    padded = with_halo(partials, (("gz", 3),), 1)
    summed = summed + (padded[:, :, :, 2:] - padded[:, :, :, :-2])
    return summed - sponge * adjoint


def body(
    terminal_adjoint,
    density,
    velocity,
    stiffness,
    sponge,
    source_shape,
    brick_level,
    brick_patch,
    patch_owner,
):
    index_x = lax.axis_index("gx")
    index_y = lax.axis_index("gy")
    index_z = lax.axis_index("gz")
    count_y = lax.axis_size("gy")
    count_z = lax.axis_size("gz")
    cells_x, cells_y, cells_z = density.shape
    own_brick = (index_x * count_y + index_y) * count_z + index_z
    patch_index = jnp.arange(patch_owner.shape[0], dtype=jnp.int32)
    own_patch = jnp.sum(jnp.where(patch_owner == own_brick, patch_index, 0))
    selector = (brick_patch.reshape(1, -1) == own_patch).astype(jnp.float32)
    own_level = brick_level[index_x, index_y, index_z]
    half_inverse = 0.5 * jnp.exp2(own_level.astype(jnp.float32))

    def apply_op(field_now):
        return apply_faces(field_now, density, velocity, stiffness, half_inverse, sponge)

    adjoint = terminal_adjoint
    section_one = adjoint + step_length * apply_op(adjoint)
    section_two = 0.75 * adjoint + 0.25 * (section_one + step_length * apply_op(section_one))
    adjoint = third * adjoint + two_thirds * (section_two + step_length * apply_op(section_two))
    weighted = adjoint * source_shape
    boxed = weighted.reshape(5, cells_x // BX, BX, cells_y // BY, BY, cells_z // BZ, BZ)
    block_now = step_length * jnp.sum(boxed, axis=(2, 4, 6)).reshape(1, -1)
    gradient = jnp.dot(
        selector,
        lax.all_gather(block_now, ("gx", "gy", "gz"), axis=0, tiled=True),
        preferred_element_type=jnp.float32,
        precision=lax.Precision.HIGHEST,
    )
    return (adjoint, gradient)


def solution(mesh):
    in_specs = (
        P(None, "gx", "gy", "gz"),
        P("gx", "gy", "gz"),
        P(None, "gx", "gy", "gz"),
        P("gx", "gy", "gz"),
        P("gx", "gy", "gz"),
        P("gx", "gy", "gz"),
        P(),
        P(),
        P(),
    )
    out_specs = (P(None, "gx", "gy", "gz"), P(("gx", "gy", "gz"), None))
    return jax.shard_map(body, mesh=mesh, in_specs=in_specs, out_specs=out_specs, check_vma=False)
```

profile of v0, /device:TPU:1, one launch (start us, length us, event | category | flops | bytes accessed | tf_op | source)
XLA Modules:
  0.0 197.1 jit_solution(8998301875433406162)
XLA Ops:
  0.6 0.0 copy-start
  0.6 1.3 dynamic_slice.3
  2.6 0.0 copy-start.1
  2.7 0.8 constant_dynamic-update-slice_fusion.9
  3.5 0.8 constant_dynamic-update-slice_fusion.4
  4.3 0.0 copy-start.2
  4.3 0.0 copy-start.4
  4.4 0.7 copy-done.2
  5.1 0.0 copy-done.4
  5.2 1.3 collective-permute-start
  6.5 8.6 %collective-permute-start.1 = (f32[5,1,8,128]{3,2,1,0:T(8,128)S(1)}, f32[5,1,8,128]{3,2,1,0:T(8,128)S(1)}, u32[]{:S(2)}, u32[]{:S(2)}) collective-permute-start(f32[5,1,8,128]{3,2,1,0:T(8,128)S(1)} %get-tuple-element.50), channel_id=1, source_target_pairs={{0,64},{64,128},{128,192},{192,256},{256,320},{320,384},{384,448},... | collective-permute-start | bytes 61448 | tf_op jit(solution)/shard_map/ppermute | solution.py:21
  15.2 16.0 %collective-permute-start.2 = (f32[5,8,1,128]{3,2,1,0:T(1,128)S(1)}, f32[5,8,1,128]{3,2,1,0:T(1,128)S(1)}, u32[]{:S(2)}, u32[]{:S(2)}) collective-permute-start(f32[5,8,1,128]{3,2,1,0:T(1,128)S(1)} %get-tuple-element.51), channel_id=1, source_target_pairs={{8,0},{16,8},{24,16},{32,24},{40,32},{48,40},{56,48},{9,1},{17,9},... | collective-permute-start | bytes 61448 | tf_op jit(solution)/shard_map/ppermute | solution.py:24
  31.1 1.9 collective-permute-start.3
  33.1 0.0 copy-start.3
  33.1 0.1 fusion.66
  33.2 1.3 collective-permute-start.4
  34.5 5.9 %collective-permute-done.4 = f32[5,8,8,1]{3,2,1,0:T(8,128)S(1)} collective-permute-done((f32[5,8,8,1]{3,2,1,0:T(8,128)S(1)}, f32[5,8,8,1]{3,2,1,0:T(8,128)S(1)}, u32[]{:S(2)}, u32[]{:S(2)}) %collective-permute-start.4) | collective-permute-done | bytes 1312 | tf_op jit(solution)/shard_map/ppermute | solution.py:24
  40.3 1.3 collective-permute-start.5
  41.7 2.2 %collective-permute-done.5 = f32[5,8,8,1]{3,2,1,0:T(8,128)S(1)} collective-permute-done((f32[5,8,8,1]{3,2,1,0:T(8,128)S(1)}, f32[5,8,8,1]{3,2,1,0:T(8,128)S(1)}, u32[]{:S(2)}, u32[]{:S(2)}) %collective-permute-start.5) | collective-permute-done | bytes 1312 | tf_op jit(solution)/shard_map/ppermute | solution.py:21
  43.9 0.0 collective-permute-done
  43.9 0.0 collective-permute-done.1
  43.9 0.0 collective-permute-done.2
  43.9 0.0 collective-permute-done.3
  43.9 0.2 fusion.24
  44.3 0.1 fusion.63
  44.4 1.3 collective-permute-start.10
  45.7 4.7 %collective-permute-start.11 = (f32[5,8,8,1]{3,2,1,0:T(8,128)S(1)}, f32[5,8,8,1]{3,2,1,0:T(8,128)S(1)}, u32[]{:S(2)}, u32[]{:S(2)}) collective-permute-start(f32[5,8,8,1]{3,2,1,0:T(8,128)S(1)} %get-tuple-element.48), channel_id=1, source_target_pairs={{0,1},{1,2},{2,3},{3,4},{4,5},{5,6},{6,7},{8,9},{9,10},{10,11},{11... | collective-permute-start | bytes 3848 | tf_op jit(solution)/shard_map/ppermute | solution.py:21
  50.5 1.3 collective-permute-start.6
  51.8 7.9 %collective-permute-start.7 = (f32[5,1,8,128]{3,2,1,0:T(8,128)S(1)}, f32[5,1,8,128]{3,2,1,0:T(8,128)S(1)}, u32[]{:S(2)}, u32[]{:S(2)}) collective-permute-start(f32[5,1,8,128]{3,2,1,0:T(8,128)S(1)} %get-tuple-element.44), channel_id=1, source_target_pairs={{0,64},{64,128},{128,192},{192,256},{256,320},{320,384},{384,448},... | collective-permute-start | bytes 61448 | tf_op jit(solution)/shard_map/ppermute | solution.py:21
  59.7 0.0 copy-start.7
  59.8 4.9 %collective-permute-start.8 = (f32[5,8,1,128]{3,2,1,0:T(1,128)S(1)}, f32[5,8,1,128]{3,2,1,0:T(1,128)S(1)}, u32[]{:S(2)}, u32[]{:S(2)}) collective-permute-start(f32[5,8,1,128]{3,2,1,0:T(1,128)S(1)} %get-tuple-element.45), channel_id=1, source_target_pairs={{8,0},{16,8},{24,16},{32,24},{40,32},{48,40},{56,48},{9,1},{17,9},... | collective-permute-start | bytes 61448 | tf_op jit(solution)/shard_map/ppermute | solution.py:24
  64.7 0.0 collective-permute-done.10
  64.7 1.9 collective-permute-start.9
  66.6 0.6 select_reduce_fusion
  67.3 0.0 collective-permute-done.11
  67.3 0.0 collective-permute-done.6
  67.3 0.0 collective-permute-done.7
  67.3 0.0 collective-permute-done.8
  67.3 0.5 collective-permute-done.9
  67.8 0.2 fusion.16
  68.2 0.1 fusion.60
  68.3 1.3 collective-permute-start.16
  69.6 4.3 %collective-permute-start.17 = (f32[5,8,8,1]{3,2,1,0:T(8,128)S(1)}, f32[5,8,8,1]{3,2,1,0:T(8,128)S(1)}, u32[]{:S(2)}, u32[]{:S(2)}) collective-permute-start(f32[5,8,8,1]{3,2,1,0:T(8,128)S(1)} %get-tuple-element.42), channel_id=1, source_target_pairs={{0,1},{1,2},{2,3},{3,4},{4,5},{5,6},{6,7},{8,9},{9,10},{10,11},{11... | collective-permute-start | bytes 3848 | tf_op jit(solution)/shard_map/ppermute | solution.py:21
  73.9 1.3 collective-permute-start.12
  75.2 7.9 %collective-permute-start.13 = (f32[5,1,8,128]{3,2,1,0:T(8,128)S(1)}, f32[5,1,8,128]{3,2,1,0:T(8,128)S(1)}, u32[]{:S(2)}, u32[]{:S(2)}) collective-permute-start(f32[5,1,8,128]{3,2,1,0:T(8,128)S(1)} %get-tuple-element.38), channel_id=1, source_target_pairs={{0,64},{64,128},{128,192},{192,256},{256,320},{320,384},{384,448},... | collective-permute-start | bytes 61448 | tf_op jit(solution)/shard_map/ppermute | solution.py:21
  83.1 0.0 copy-start.6
  83.2 2.9 %collective-permute-start.14 = (f32[5,8,1,128]{3,2,1,0:T(1,128)S(1)}, f32[5,8,1,128]{3,2,1,0:T(1,128)S(1)}, u32[]{:S(2)}, u32[]{:S(2)}) collective-permute-start(f32[5,8,1,128]{3,2,1,0:T(1,128)S(1)} %get-tuple-element.39), channel_id=1, source_target_pairs={{8,0},{16,8},{24,16},{32,24},{40,32},{48,40},{56,48},{9,1},{17,9},... | collective-permute-start | bytes 61448 | tf_op jit(solution)/shard_map/ppermute | solution.py:24
  86.1 0.0 collective-permute-done.16
  86.1 3.8 %collective-permute-start.15 = (f32[5,8,1,128]{3,2,1,0:T(1,128)S(1)}, f32[5,8,1,128]{3,2,1,0:T(1,128)S(1)}, u32[]{:S(2)}, u32[]{:S(2)}) collective-permute-start(f32[5,8,1,128]{3,2,1,0:T(1,128)S(1)} %get-tuple-element.40), channel_id=1, source_target_pairs={{0,8},{8,16},{16,24},{24,32},{32,40},{40,48},{48,56},{1,9},{9,17},... | collective-permute-start | bytes 61448 | tf_op jit(solution)/shard_map/ppermute | solution.py:21
  89.9 0.7 broadcast_compare_fusion
  90.6 0.0 copy-start.5
  90.6 0.1 copy.13
  90.7 0.1 reshape.43
  90.8 0.0 collective-permute-done.17
  90.8 0.0 collective-permute-done.12
  90.8 0.0 collective-permute-done.14
  90.8 0.0 collective-permute-done.15
  90.8 0.5 copy-done.5
  91.3 0.9 multiply_reduce_fusion
  92.2 0.1 reduce_sum.27
  92.3 0.1 reduce_sum.28
  92.4 0.1 reshape.40
  92.5 103.9 %all-gather = f32[1024,1,40]{2,1,0:T(1,128)S(1)} all-gather(f32[1,1,40]{2,1,0:T(1,128)S(1)} %reshape.40), channel_id=1, replica_groups=mesh['gx'=16,'gy'=8,'gz'=8] {'gx','gy','gz'}, dimensions={0}, use_global_device_ids=true | all-gather | bytes 164000 | tf_op jit(solution)/shard_map/all_gather | solution.py:89
  196.3 0.8 fusion.67
  (44 shorter events, 0.5 us)
Async XLA Ops:
  0.6 2.9 %copy-start = (f32[3,8,8,128]{3,2,1,0:T(8,128)S(1)}, f32[3,8,8,128]{3,2,1,0:T(8,128)}, u32[]{:S(2)}) copy-start(f32[3,8,8,128]{3,2,1,0:T(8,128)} %param.11) | copy-start | bytes 294916
  2.6 1.6 copy-start.1
  4.3 0.8 copy-start.2
  4.3 0.8 copy-start.4
  5.2 38.7 %collective-permute-start = (f32[5,1,8,128]{3,2,1,0:T(8,128)S(1)}, f32[5,1,8,128]{3,2,1,0:T(8,128)S(1)}, u32[]{:S(2)}, u32[]{:S(2)}) collective-permute-start(f32[5,1,8,128]{3,2,1,0:T(8,128)S(1)} %get-tuple-element.49), channel_id=1, source_target_pairs={{64,0},{128,64},{192,128},{256,192},{320,256},{384,320},{448,384},... | collective-permute-start | bytes 61448 | tf_op jit(solution)/shard_map/ppermute | solution.py:24
  6.5 37.4 %collective-permute-start.1 = (f32[5,1,8,128]{3,2,1,0:T(8,128)S(1)}, f32[5,1,8,128]{3,2,1,0:T(8,128)S(1)}, u32[]{:S(2)}, u32[]{:S(2)}) collective-permute-start(f32[5,1,8,128]{3,2,1,0:T(8,128)S(1)} %get-tuple-element.50), channel_id=1, source_target_pairs={{0,64},{64,128},{128,192},{192,256},{256,320},{320,384},{384,448},... | collective-permute-start | bytes 61448 | tf_op jit(solution)/shard_map/ppermute | solution.py:21
  15.2 28.7 %collective-permute-start.2 = (f32[5,8,1,128]{3,2,1,0:T(1,128)S(1)}, f32[5,8,1,128]{3,2,1,0:T(1,128)S(1)}, u32[]{:S(2)}, u32[]{:S(2)}) collective-permute-start(f32[5,8,1,128]{3,2,1,0:T(1,128)S(1)} %get-tuple-element.51), channel_id=1, source_target_pairs={{8,0},{16,8},{24,16},{32,24},{40,32},{48,40},{56,48},{9,1},{17,9},... | collective-permute-start | bytes 61448 | tf_op jit(solution)/shard_map/ppermute | solution.py:24
  31.1 12.8 %collective-permute-start.3 = (f32[5,8,1,128]{3,2,1,0:T(1,128)S(1)}, f32[5,8,1,128]{3,2,1,0:T(1,128)S(1)}, u32[]{:S(2)}, u32[]{:S(2)}) collective-permute-start(f32[5,8,1,128]{3,2,1,0:T(1,128)S(1)} %get-tuple-element.52), channel_id=1, source_target_pairs={{0,8},{8,16},{16,24},{24,32},{32,40},{40,48},{48,56},{1,9},{9,17},... | collective-permute-start | bytes 61448 | tf_op jit(solution)/shard_map/ppermute | solution.py:21
  33.1 10.8 %copy-start.3 = (f32[8,8,128]{2,1,0:T(8,128)S(1)}, f32[8,8,128]{2,1,0:T(8,128)}, u32[]{:S(2)}) copy-start(f32[8,8,128]{2,1,0:T(8,128)} %param.13) | copy-start | bytes 98308
  33.2 7.2 %collective-permute-start.4 = (f32[5,8,8,1]{3,2,1,0:T(8,128)S(1)}, f32[5,8,8,1]{3,2,1,0:T(8,128)S(1)}, u32[]{:S(2)}, u32[]{:S(2)}) collective-permute-start(f32[5,8,8,1]{3,2,1,0:T(8,128)S(1)} %get-tuple-element.53), channel_id=1, source_target_pairs={{1,0},{2,1},{3,2},{4,3},{5,4},{6,5},{7,6},{9,8},{10,9},{11,10},{12... | collective-permute-start | bytes 3848 | tf_op jit(solution)/shard_map/ppermute | solution.py:24
  40.3 3.5 %collective-permute-start.5 = (f32[5,8,8,1]{3,2,1,0:T(8,128)S(1)}, f32[5,8,8,1]{3,2,1,0:T(8,128)S(1)}, u32[]{:S(2)}, u32[]{:S(2)}) collective-permute-start(f32[5,8,8,1]{3,2,1,0:T(8,128)S(1)} %get-tuple-element.54), channel_id=1, source_target_pairs={{0,1},{1,2},{2,3},{3,4},{4,5},{5,6},{6,7},{8,9},{9,10},{10,11},{11... | collective-permute-start | bytes 3848 | tf_op jit(solution)/shard_map/ppermute | solution.py:21
  44.4 20.3 %collective-permute-start.10 = (f32[5,8,8,1]{3,2,1,0:T(8,128)S(1)}, f32[5,8,8,1]{3,2,1,0:T(8,128)S(1)}, u32[]{:S(2)}, u32[]{:S(2)}) collective-permute-start(f32[5,8,8,1]{3,2,1,0:T(8,128)S(1)} %get-tuple-element.47), channel_id=1, source_target_pairs={{1,0},{2,1},{3,2},{4,3},{5,4},{6,5},{7,6},{9,8},{10,9},{11,10},{12... | collective-permute-start | bytes 3848 | tf_op jit(solution)/shard_map/ppermute | solution.py:24
  45.7 21.5 %collective-permute-start.11 = (f32[5,8,8,1]{3,2,1,0:T(8,128)S(1)}, f32[5,8,8,1]{3,2,1,0:T(8,128)S(1)}, u32[]{:S(2)}, u32[]{:S(2)}) collective-permute-start(f32[5,8,8,1]{3,2,1,0:T(8,128)S(1)} %get-tuple-element.48), channel_id=1, source_target_pairs={{0,1},{1,2},{2,3},{3,4},{4,5},{5,6},{6,7},{8,9},{9,10},{10,11},{11... | collective-permute-start | bytes 3848 | tf_op jit(solution)/shard_map/ppermute | solution.py:21
  50.5 16.8 %collective-permute-start.6 = (f32[5,1,8,128]{3,2,1,0:T(8,128)S(1)}, f32[5,1,8,128]{3,2,1,0:T(8,128)S(1)}, u32[]{:S(2)}, u32[]{:S(2)}) collective-permute-start(f32[5,1,8,128]{3,2,1,0:T(8,128)S(1)} %get-tuple-element.43), channel_id=1, source_target_pairs={{64,0},{128,64},{192,128},{256,192},{320,256},{384,320},{448,384},... | collective-permute-start | bytes 61448 | tf_op jit(solution)/shard_map/ppermute | solution.py:24
  51.8 15.5 %collective-permute-start.7 = (f32[5,1,8,128]{3,2,1,0:T(8,128)S(1)}, f32[5,1,8,128]{3,2,1,0:T(8,128)S(1)}, u32[]{:S(2)}, u32[]{:S(2)}) collective-permute-start(f32[5,1,8,128]{3,2,1,0:T(8,128)S(1)} %get-tuple-element.44), channel_id=1, source_target_pairs={{0,64},{64,128},{128,192},{192,256},{256,320},{320,384},{384,448},... | collective-permute-start | bytes 61448 | tf_op jit(solution)/shard_map/ppermute | solution.py:21
  59.7 6.9 %copy-start.7 = (s32[1024]{0:T(1024)S(1)}, s32[1024]{0:T(1024)}, u32[]{:S(2)}) copy-start(s32[1024]{0:T(1024)} %param.17) | copy-start | bytes 12292
  59.8 7.5 %collective-permute-start.8 = (f32[5,8,1,128]{3,2,1,0:T(1,128)S(1)}, f32[5,8,1,128]{3,2,1,0:T(1,128)S(1)}, u32[]{:S(2)}, u32[]{:S(2)}) collective-permute-start(f32[5,8,1,128]{3,2,1,0:T(1,128)S(1)} %get-tuple-element.45), channel_id=1, source_target_pairs={{8,0},{16,8},{24,16},{32,24},{40,32},{48,40},{56,48},{9,1},{17,9},... | collective-permute-start | bytes 61448 | tf_op jit(solution)/shard_map/ppermute | solution.py:24
  64.7 3.1 %collective-permute-start.9 = (f32[5,8,1,128]{3,2,1,0:T(1,128)S(1)}, f32[5,8,1,128]{3,2,1,0:T(1,128)S(1)}, u32[]{:S(2)}, u32[]{:S(2)}) collective-permute-start(f32[5,8,1,128]{3,2,1,0:T(1,128)S(1)} %get-tuple-element.46), channel_id=1, source_target_pairs={{0,8},{8,16},{16,24},{24,32},{32,40},{40,48},{48,56},{1,9},{9,17},... | collective-permute-start | bytes 61448 | tf_op jit(solution)/shard_map/ppermute | solution.py:21
  68.3 17.8 %collective-permute-start.16 = (f32[5,8,8,1]{3,2,1,0:T(8,128)S(1)}, f32[5,8,8,1]{3,2,1,0:T(8,128)S(1)}, u32[]{:S(2)}, u32[]{:S(2)}) collective-permute-start(f32[5,8,8,1]{3,2,1,0:T(8,128)S(1)} %get-tuple-element.41), channel_id=1, source_target_pairs={{1,0},{2,1},{3,2},{4,3},{5,4},{6,5},{7,6},{9,8},{10,9},{11,10},{12... | collective-permute-start | bytes 3848 | tf_op jit(solution)/shard_map/ppermute | solution.py:24
  69.6 21.2 %collective-permute-start.17 = (f32[5,8,8,1]{3,2,1,0:T(8,128)S(1)}, f32[5,8,8,1]{3,2,1,0:T(8,128)S(1)}, u32[]{:S(2)}, u32[]{:S(2)}) collective-permute-start(f32[5,8,8,1]{3,2,1,0:T(8,128)S(1)} %get-tuple-element.42), channel_id=1, source_target_pairs={{0,1},{1,2},{2,3},{3,4},{4,5},{5,6},{6,7},{8,9},{9,10},{10,11},{11... | collective-permute-start | bytes 3848 | tf_op jit(solution)/shard_map/ppermute | solution.py:21
  73.9 16.9 %collective-permute-start.12 = (f32[5,1,8,128]{3,2,1,0:T(8,128)S(1)}, f32[5,1,8,128]{3,2,1,0:T(8,128)S(1)}, u32[]{:S(2)}, u32[]{:S(2)}) collective-permute-start(f32[5,1,8,128]{3,2,1,0:T(8,128)S(1)} %get-tuple-element.37), channel_id=1, source_target_pairs={{64,0},{128,64},{192,128},{256,192},{320,256},{384,320},{448,384},... | collective-permute-start | bytes 61448 | tf_op jit(solution)/shard_map/ppermute | solution.py:24
  75.2 15.6 %collective-permute-start.13 = (f32[5,1,8,128]{3,2,1,0:T(8,128)S(1)}, f32[5,1,8,128]{3,2,1,0:T(8,128)S(1)}, u32[]{:S(2)}, u32[]{:S(2)}) collective-permute-start(f32[5,1,8,128]{3,2,1,0:T(8,128)S(1)} %get-tuple-element.38), channel_id=1, source_target_pairs={{0,64},{64,128},{128,192},{192,256},{256,320},{320,384},{384,448},... | collective-permute-start | bytes 61448 | tf_op jit(solution)/shard_map/ppermute | solution.py:21
  83.1 6.8 %copy-start.6 = (s32[16,8,8]{0,2,1:T(8,128)S(1)}, s32[16,8,8]{0,2,1:T(8,128)}, u32[]{:S(2)}) copy-start(s32[16,8,8]{0,2,1:T(8,128)} %param.16) | copy-start | bytes 12292
  83.2 7.7 %collective-permute-start.14 = (f32[5,8,1,128]{3,2,1,0:T(1,128)S(1)}, f32[5,8,1,128]{3,2,1,0:T(1,128)S(1)}, u32[]{:S(2)}, u32[]{:S(2)}) collective-permute-start(f32[5,8,1,128]{3,2,1,0:T(1,128)S(1)} %get-tuple-element.39), channel_id=1, source_target_pairs={{8,0},{16,8},{24,16},{32,24},{40,32},{48,40},{56,48},{9,1},{17,9},... | collective-permute-start | bytes 61448 | tf_op jit(solution)/shard_map/ppermute | solution.py:24
  86.1 4.7 %collective-permute-start.15 = (f32[5,8,1,128]{3,2,1,0:T(1,128)S(1)}, f32[5,8,1,128]{3,2,1,0:T(1,128)S(1)}, u32[]{:S(2)}, u32[]{:S(2)}) collective-permute-start(f32[5,8,1,128]{3,2,1,0:T(1,128)S(1)} %get-tuple-element.40), channel_id=1, source_target_pairs={{0,8},{8,16},{16,24},{24,32},{32,40},{40,48},{48,56},{1,9},{9,17},... | collective-permute-start | bytes 61448 | tf_op jit(solution)/shard_map/ppermute | solution.py:21
  90.6 0.8 copy-start.5
where the time goes:
time: 198 us; the launch traced here: 197 us
  blocking collectives  104 us (53%)
  starting transfers between devices  73.8 us (37%)
  waiting for transfers between devices  8.62 us (4%)
  other arithmetic  4.71 us (2%)
  local copies, waits for them, and re-layouts  3.33 us (2%)
  between operations  2 us (1%)
    all_gather x1, blocking collectives, body(): lax.all_gather(block_now, ('gx', 'gy', 'gz'), axis=0, tiled=True)  104 us
    ppermute x9, starting transfers between devices, with_halo(): lax.ppermute(lax.slice_in_dim(block, block.shape[dim] - width, None, axis...  42.3 us
    ppermute x9, starting transfers between devices, with_halo(): lax.ppermute(lax.slice_in_dim(block, 0, width, axis=dim), axis, backward)  31.5 us
    ppermute x9, waiting for transfers between devices, with_halo(): lax.ppermute(lax.slice_in_dim(block, 0, width, axis=dim), axis, backward)  5.89 us
  transfers between devices with their start and end apart: 18, of which 3 were waited for; matrix products, arithmetic and copies ran while one was open for 1% of the time, Pallas kernels for 0%

commit v1 on v0

v1 whole, which is shorter than its diff:
```python
import functools

import jax
import jax.numpy as jnp
from jax import lax
from jax.experimental import pallas as pl
from jax.experimental.pallas import tpu as pltpu
from jax.sharding import PartitionSpec as P

MESH = pl.DeviceIdType.MESH
F = 5
X = 8
Y = 8
Z = 128
BZ = 16
BOXES = Z // BZ
STAGES = 3
step_length = 0.14
third = 1.0 / 3.0
AXES = ("gx", "gy", "gz")


def kernel(
    sizes,
    level_ref,
    patch_ref,
    owner_ref,
    adjoint_hbm,
    density_hbm,
    velocity_hbm,
    stiffness_hbm,
    sponge_hbm,
    source_hbm,
    out_hbm,
    grad_ref,
    fields,
    density,
    velocity,
    stiffness,
    sponge,
    source,
    speed,
    pull,
    push,
    inverse,
    damp,
    flux_x,
    flux_y,
    send_y,
    send_z,
    halo_x,
    halo_y,
    halo_z,
    result,
    row_send,
    row_recv,
    cell_send,
    cell_recv,
    load_sem,
    store_sem,
    halo_send_sem,
    halo_recv_sem,
    row_send_sem,
    row_recv_sem,
    cell_send_sem,
    cell_recv_sem,
):
    n_gx, n_gy, n_gz = sizes
    gx, gy, gz = (lax.axis_index(axis) for axis in AXES)
    half = lax.rem(gx, 2)
    plane = lax.div(gx, 2)
    n_plane = n_gx // 2
    n_row = 2 * n_gy
    n_cell = n_plane * n_gz
    my_row = half * n_gy + gy
    my_cell = plane * n_gz + gz

    def row_device(t):
        return (plane * 2 + lax.div(t, n_gy), lax.rem(t, n_gy), gz)

    def cell_device(t):
        return (lax.div(t, n_gz) * 2 + half, gy, lax.rem(t, n_gz))

    barrier = pltpu.get_barrier_semaphore()
    me = (gx, gy, gz)
    ups, downs, has_up, has_down = [], [], [], []
    for d in range(3):
        up, down = list(me), list(me)
        up[d] = jnp.minimum(me[d] + 1, sizes[d] - 1)
        down[d] = jnp.maximum(me[d] - 1, 0)
        ups.append(tuple(up))
        downs.append(tuple(down))
        has_up.append(me[d] < sizes[d] - 1)
        has_down.append(me[d] > 0)
    expected = jnp.int32(n_row - 1 + n_cell - 1)
    for d in range(3):
        for has, to in ((has_up[d], ups[d]), (has_down[d], downs[d])):
            expected = expected + jnp.where(has, 1, 0)

            @pl.when(has)
            def _(to=to):
                pl.semaphore_signal(barrier, inc=1, device_id=to, device_id_type=MESH)

    loads = []
    for i, (src, dst) in enumerate(
        (
            (density_hbm, density),
            (velocity_hbm, velocity),
            (stiffness_hbm, stiffness),
            (sponge_hbm, sponge),
            (adjoint_hbm, fields.at[0]),
            (source_hbm, source),
        )
    ):
        copy = pltpu.make_async_copy(src, dst, load_sem.at[i])
        copy.start()
        loads.append(copy)

    def greet_row(r, c):
        pl.semaphore_signal(
            barrier, inc=1, device_id=row_device(lax.rem(my_row + r, n_row)), device_id_type=MESH
        )
        return c

    lax.fori_loop(1, n_row, greet_row, 0)

    def greet_cell(r, c):
        pl.semaphore_signal(
            barrier, inc=1, device_id=cell_device(lax.rem(my_cell + r, n_cell)), device_id_type=MESH
        )
        return c

    lax.fori_loop(1, n_cell, greet_cell, 0)

    for d, halo in enumerate((halo_x, halo_y, halo_z)):
        for side, has in ((0, has_down[d]), (1, has_up[d])):

            @pl.when(jnp.logical_not(has))
            def _(halo=halo, side=side):
                for k in range(STAGES):
                    halo[k, side] = jnp.zeros(halo.shape[2:], jnp.float32)

    level = level_ref[gy, gz, gx]
    scale = 0.5 * step_length * lax.shift_left(jnp.int32(1), level).astype(jnp.float32)
    for copy in loads[:4]:
        copy.wait()
    for x in range(X):
        rho = density[x]
        speed[:, x] = scale * velocity[:, x]
        pull[x] = scale * rho
        push[x] = scale * stiffness[x]
        inverse[x] = scale / rho
        damp[x] = 1.0 - step_length * sponge[x]
    loads[4].wait()

    sub = lax.broadcasted_iota(jnp.int32, (Y, Z), 0)
    lane = lax.broadcasted_iota(jnp.int32, (Y, Z), 1)
    first_y, last_y = sub == 0, sub == Y - 1
    first_z, last_z = lane == 0, lane == Z - 1

    def flux(v, joint, x, d):
        c = speed[d, x]
        q = [c * v[f] for f in range(F)]
        q[1 + d] = q[1 + d] + joint
        q[4] = q[4] + inverse[x] * v[1 + d]
        return q

    def joint_term(v, x):
        return pull[x] * v[0] + push[x] * v[4]

    def halo_copy(k, d, side):
        src = (
            flux_x.at[k, (X - 1) * side],
            send_y.at[k, side],
            send_z.at[k, side],
        )[d]
        dst = (halo_x, halo_y, halo_z)[d].at[k, 1 - side]
        return pltpu.make_async_remote_copy(
            src_ref=src,
            dst_ref=dst,
            send_sem=halo_send_sem.at[k, d, side],
            recv_sem=halo_recv_sem.at[k, d, 1 - side],
            device_id=ups[d] if side else downs[d],
            device_id_type=MESH,
        )

    def send_halo(k, d):
        for side, has in ((1, has_up[d]), (0, has_down[d])):

            @pl.when(has)
            def _(side=side):
                halo_copy(k, d, side).start()

    def wait_halo(k, d):
        for side, has in ((1, has_down[d]), (0, has_up[d])):

            @pl.when(has)
            def _(side=side):
                halo_copy(k, d, side).wait_recv()

    for k in range(STAGES):
        for x in (0, X - 1):
            v = [fields[k, f, x] for f in range(F)]
            q = flux(v, joint_term(v, x), x, 0)
            for f in range(F):
                flux_x[k, x, f] = q[f]
        if k == 0:
            pl.semaphore_wait(barrier, expected)
        send_halo(k, 0)
        packs = [jnp.zeros((Y, Z), jnp.float32), jnp.zeros((Y, Z), jnp.float32)]
        for x in range(X):
            v = [fields[k, f, x] for f in range(F)]
            joint = joint_term(v, x)
            if 0 < x < X - 1:
                q = flux(v, joint, x, 0)
                for f in range(F):
                    flux_x[k, x, f] = q[f]
            q = flux(v, joint, x, 2)
            for f in range(F):
                here = lane == f * X + x
                packs[0] = jnp.where(here, jnp.broadcast_to(q[f][:, 0:1], (Y, Z)), packs[0])
                packs[1] = jnp.where(here, jnp.broadcast_to(q[f][:, Z - 1 : Z], (Y, Z)), packs[1])
                fields[k + 1, f, x] = (
                    damp[x] * v[f]
                    + jnp.where(last_z, 0.0, pltpu.roll(q[f], Z - 1, 1))
                    - jnp.where(first_z, 0.0, pltpu.roll(q[f], 1, 1))
                )
            q = flux(v, joint, x, 1)
            for f in range(F):
                flux_y[k, f, pl.ds(x * Y, Y), :] = q[f]
                fields[k + 1, f, x] += jnp.where(last_y, 0.0, pltpu.roll(q[f], Y - 1, 0)) - jnp.where(
                    first_y, 0.0, pltpu.roll(q[f], 1, 0)
                )
        for side in range(2):
            send_z[k, side] = packs[side]
        send_halo(k, 2)
        for f in range(F):
            for side in range(2):
                send_y[k, side, f] = flux_y[k, f, pl.ds((Y - 1) * side, X, stride=Y), :]
        send_halo(k, 1)
        for x in range(X):
            for f in range(F):
                if x == 0:
                    fields[k + 1, f, x] += flux_x[k, x + 1, f]
                elif x == X - 1:
                    fields[k + 1, f, x] -= flux_x[k, x - 1, f]
                else:
                    fields[k + 1, f, x] += flux_x[k, x + 1, f] - flux_x[k, x - 1, f]
        wait_halo(k, 1)
        wait_halo(k, 2)
        low_z, high_z = halo_z[k, 0], halo_z[k, 1]
        for f in range(F):
            low_y, high_y = halo_y[k, 0, f], halo_y[k, 1, f]
            for x in range(X):
                at = f * X + x
                delta = jnp.where(
                    last_y,
                    jnp.broadcast_to(high_y[x : x + 1], (Y, Z)),
                    jnp.where(first_y, -jnp.broadcast_to(low_y[x : x + 1], (Y, Z)), 0.0),
                )
                delta += jnp.where(
                    last_z,
                    jnp.broadcast_to(high_z[:, at : at + 1], (Y, Z)),
                    jnp.where(first_z, -jnp.broadcast_to(low_z[:, at : at + 1], (Y, Z)), 0.0),
                )
                fields[k + 1, f, x] += delta
        wait_halo(k, 0)
        for f in range(F):
            fields[k + 1, f, 0] -= halo_x[k, 0, f]
            fields[k + 1, f, X - 1] += halo_x[k, 1, f]

    loads[5].wait()
    lines = []
    for f in range(F):
        total = jnp.zeros((Y, Z), jnp.float32)
        for x in range(X):
            value = third * fields[0, f, x] + 0.5 * fields[1, f, x] + (0.5 * third) * fields[3, f, x]
            result[f, x] = value
            total += value * source[x]
        lines.append(jnp.sum(total, axis=0, keepdims=True))
    store = pltpu.make_async_copy(result, out_hbm, store_sem)
    store.start()

    row_lane = lax.broadcasted_iota(jnp.int32, (1, Z), 1)
    block = jnp.zeros((1, Z), jnp.float32)
    for f in range(F):
        line = lines[f]
        for shift in (1, 2, 4, 8):
            line = line + pltpu.roll(line, Z - shift, 1)
        if f:
            line = pltpu.roll(line, f, 1)
        block = jnp.where(lax.rem(row_lane, BZ) == f, line, block)
    block = step_length * block

    def owner_of(i, j, k):
        return owner_ref[patch_ref[j, k, i]]

    def split_owner(o):
        ox = lax.div(o, n_gy * n_gz)
        oy = lax.rem(lax.div(o, n_gz), n_gy)
        oz = lax.rem(o, n_gz)
        return lax.rem(ox, 2) * n_gy + oy, lax.div(ox, 2) * n_gz + oz

    to_row, _ = split_owner(owner_of(gx, gy, gz))
    for t in range(n_row):
        row_send[t] = jnp.where(to_row == t, block, 0.0)

    def row_copy(r):
        t = lax.rem(my_row + r, n_row)
        return pltpu.make_async_remote_copy(
            src_ref=row_send.at[t],
            dst_ref=row_recv.at[my_row],
            send_sem=row_send_sem.at[r],
            recv_sem=row_recv_sem.at[r],
            device_id=row_device(t),
            device_id_type=MESH,
        )

    def loop(n, body):
        def step(r, c):
            body(r)
            return c

        lax.fori_loop(1, n, step, 0)

    loop(n_row, lambda r: row_copy(r).start())
    row_recv[my_row] = row_send[my_row]

    target = jnp.full((1, n_row), -1, jnp.int32)
    at = lax.broadcasted_iota(jnp.int32, (1, n_row), 1)
    for t in range(n_row):
        _, cell = split_owner(owner_of(plane * 2 + t // n_gy, t % n_gy, gz))
        target = jnp.where(at == t, cell, target)
    choose = (lax.broadcasted_iota(jnp.int32, (n_cell, n_row), 0) == target).astype(jnp.float32)
    spread_to = lax.broadcasted_iota(jnp.int32, (Z, Z), 1)
    spread = (
        lax.broadcasted_iota(jnp.int32, (Z, Z), 0)
        == BZ * lax.rem(spread_to, BOXES) + lax.div(spread_to, BOXES)
    ).astype(jnp.float32)

    loop(n_row, lambda r: row_copy(r).wait_recv())
    rows = row_recv[...].reshape(n_row, Z)
    cells = jnp.dot(
        choose, rows, preferred_element_type=jnp.float32, precision=lax.Precision.HIGHEST
    )
    for t in range(n_cell):
        cell_send[t] = cells[t : t + 1]

    def cell_copy(r):
        t = lax.rem(my_cell + r, n_cell)
        return pltpu.make_async_remote_copy(
            src_ref=cell_send.at[t],
            dst_ref=cell_recv.at[my_cell],
            send_sem=cell_send_sem.at[r],
            recv_sem=cell_recv_sem.at[r],
            device_id=cell_device(t),
            device_id_type=MESH,
        )

    loop(n_cell, lambda r: cell_copy(r).start())
    cell_recv[my_cell] = cell_send[my_cell]
    loop(n_cell, lambda r: cell_copy(r).wait_recv())
    own = jnp.sum(cell_recv[...].reshape(n_cell, Z), axis=0, keepdims=True)
    ordered = jnp.dot(
        own, spread, preferred_element_type=jnp.float32, precision=lax.Precision.HIGHEST
    )
    grad_ref[...] = ordered[:, : F * BOXES]

    for k in range(STAGES):
        for d in range(3):
            for side, has in ((1, has_up[d]), (0, has_down[d])):

                @pl.when(has)
                def _(side=side, k=k, d=d):
                    halo_copy(k, d, side).wait_send()

    loop(n_row, lambda r: row_copy(r).wait_send())
    loop(n_cell, lambda r: cell_copy(r).wait_send())
    store.wait()


def solution(mesh):
    sizes = tuple(mesh.shape[axis] for axis in AXES)
    n_row = 2 * sizes[1]
    n_cell = sizes[0] // 2 * sizes[2]

    def body(
        terminal_adjoint,
        density,
        velocity,
        stiffness,
        sponge,
        source_shape,
        brick_level,
        brick_patch,
        patch_owner,
    ):
        f32 = jnp.float32
        smem = pl.BlockSpec(memory_space=pltpu.SMEM)
        hbm = pl.BlockSpec(memory_space=pl.ANY)
        return pl.pallas_call(
            functools.partial(kernel, sizes),
            out_shape=(
                jax.ShapeDtypeStruct((F, X, Y, Z), f32),
                jax.ShapeDtypeStruct((1, F * BOXES), f32),
            ),
            in_specs=[smem] * 3 + [hbm] * 6,
            out_specs=(hbm, pl.BlockSpec(memory_space=pltpu.VMEM)),
            scratch_shapes=[
                pltpu.VMEM((STAGES + 1, F, X, Y, Z), f32),
                pltpu.VMEM((X, Y, Z), f32),
                pltpu.VMEM((3, X, Y, Z), f32),
                pltpu.VMEM((X, Y, Z), f32),
                pltpu.VMEM((X, Y, Z), f32),
                pltpu.VMEM((X, Y, Z), f32),
                pltpu.VMEM((3, X, Y, Z), f32),
                pltpu.VMEM((X, Y, Z), f32),
                pltpu.VMEM((X, Y, Z), f32),
                pltpu.VMEM((X, Y, Z), f32),
                pltpu.VMEM((X, Y, Z), f32),
                pltpu.VMEM((STAGES, X, F, Y, Z), f32),
                pltpu.VMEM((STAGES, F, X * Y, Z), f32),
                pltpu.VMEM((STAGES, 2, F, X, Z), f32),
                pltpu.VMEM((STAGES, 2, Y, Z), f32),
                pltpu.VMEM((STAGES, 2, F, Y, Z), f32),
                pltpu.VMEM((STAGES, 2, F, X, Z), f32),
                pltpu.VMEM((STAGES, 2, Y, Z), f32),
                pltpu.VMEM((F, X, Y, Z), f32),
                pltpu.VMEM((n_row, 1, Z), f32),
                pltpu.VMEM((n_row, 1, Z), f32),
                pltpu.VMEM((n_cell, 1, Z), f32),
                pltpu.VMEM((n_cell, 1, Z), f32),
                pltpu.SemaphoreType.DMA((6,)),
                pltpu.SemaphoreType.DMA,
                pltpu.SemaphoreType.DMA((STAGES, 3, 2)),
                pltpu.SemaphoreType.DMA((STAGES, 3, 2)),
                pltpu.SemaphoreType.DMA((n_row,)),
                pltpu.SemaphoreType.DMA((n_row,)),
                pltpu.SemaphoreType.DMA((n_cell,)),
                pltpu.SemaphoreType.DMA((n_cell,)),
            ],
            compiler_params=pltpu.CompilerParams(collective_id=0, has_side_effects=True),
        )(
            jnp.transpose(brick_level, (1, 2, 0)),
            jnp.transpose(brick_patch, (1, 2, 0)),
            patch_owner,
            terminal_adjoint,
            density,
            velocity,
            stiffness,
            sponge,
            source_shape,
        )

    in_specs = (
        P(None, "gx", "gy", "gz"),
        P("gx", "gy", "gz"),
        P(None, "gx", "gy", "gz"),
        P("gx", "gy", "gz"),
        P("gx", "gy", "gz"),
        P("gx", "gy", "gz"),
        P(),
        P(),
        P(),
    )
    out_specs = (P(None, "gx", "gy", "gz"), P(AXES, None))
    return jax.shard_map(body, mesh=mesh, in_specs=in_specs, out_specs=out_specs, check_vma=False)
```

time: 198 us -> 62.2 us (0.31)
  blocking collectives: 104 us -> 0 us
  starting transfers between devices: 73.8 us -> 0 us
  Pallas kernels: 0 us -> 59.2 us
  waiting for transfers between devices: 8.62 us -> 0 us
  other arithmetic: 4.71 us -> 0 us
    all_gather x1 -> x0, blocking collectives: 104 us -> none  [body(): lax.all_gather(block_now, ('gx', 'gy', 'gz'), axis=0, tiled=True)]
    ppermute x18 -> x0, starting transfers between devices: 73.8 us -> none  [the longest x9 42.3 us: with_halo(): lax.ppermute(lax.slice_in_dim(block, block.shape[dim] - width, None, axis...]
    pallas_call x0 -> x1, Pallas kernels: none -> 59.2 us  [body(): pl.pallas_call(functools.partial(kernel, sizes), out_shape=(jax.ShapeDtyp...]
    ppermute x18 -> x0, waiting for transfers between devices: 8.62 us -> none  [the longest x9 5.89 us: with_halo(): lax.ppermute(lax.slice_in_dim(block, 0, width, axis=dim), axis, backward)]
  transfers between devices with their start and end apart: 18 -> 0, of which waited for: 3 -> 0; matrix products, arithmetic and copies ran while one was open for 1% -> 0% of each run, Pallas kernels for 0% -> 0%
where the time goes in v1:
time: 62.2 us; the launch traced here: 61.9 us
  Pallas kernels  59.2 us (95%)
  local copies, waits for them, and re-layouts  2.11 us (3%)
  between operations  0.65 us (1%)
    pallas_call x1, Pallas kernels, body(): pl.pallas_call(functools.partial(kernel, sizes), out_shape=(jax.ShapeDtyp...  59.2 us
    unnamed x4, local copies, waits for them, and re-layouts  2.11 us

profile of v1, /device:TPU:1, one launch (start us, length us, event | category | flops | bytes accessed | tf_op | source)
XLA Modules:
  0.0 61.9 jit_solution(16567646039103275270)
XLA Ops:
  0.6 59.2 %shard_map.104 = (f32[5,8,8,128]{3,2,1,0:T(8,128)}, f32[1,40]{1,0:T(1,128)}) custom-call(s32[8,8,16]{2,1,0:T(8,128)} %bitcast.2, s32[8,8,16]{2,1,0:T(8,128)} %bitcast.3, s32[1024]{0:T(1024)} %owner_ref.1, f32[5,8,8,128]{3,2,1,0:T(8,128)} %adjoint_hbm.1, f32[8,8,128]{2,1,0:T(8,128)} %density_hbm.1, f32[3,8,8,128]{3,2,1,0:T(8,128)} %velocity_hbm.1, ...), custom_call_target="tpu_custom_call" | custom-call | tf_op jit(solution)/shard_map/pallas_call | solution.py:401
  59.8 0.0 copy-start
  59.8 1.6 %copy.13 = f32[5,8,8,128]{3,2,1,0:T(8,128)} copy(f32[5,8,8,128]{3,2,1,0:T(8,128)} %get-tuple-element.4) | data formatting | bytes 327680
  61.4 0.0 copy-done
  61.4 0.5 copy.14
Async XLA Ops:
  59.8 1.6 %copy-start = (f32[1,40]{1,0:T(1,128)S(1)}, f32[1,40]{1,0:T(1,128)}, u32[]{:S(2)}) copy-start(f32[1,40]{1,0:T(1,128)} %get-tuple-element.5) | copy-start | bytes 484

commit v2 on v1

v2 whole, which is shorter than its diff:
```python
import functools

import jax
import jax.numpy as jnp
from jax import lax
from jax.experimental import pallas as pl
from jax.experimental.pallas import tpu as pltpu
from jax.sharding import PartitionSpec as P

MESH = pl.DeviceIdType.MESH
F = 5
X = 8
Y = 8
Z = 128
BZ = 16
BOXES = Z // BZ
TILE = 8
STAGES = 3
step_length = 0.14
third = 1.0 / 3.0
AXES = ("gx", "gy", "gz")


def kernel(
    sizes,
    level_ref,
    patch_ref,
    owner_ref,
    adjoint_hbm,
    density_hbm,
    velocity_hbm,
    stiffness_hbm,
    sponge_hbm,
    source_hbm,
    out_hbm,
    grad_ref,
    fields,
    density,
    velocity,
    stiffness,
    sponge,
    source,
    speed,
    pull,
    push,
    inverse,
    damp,
    flux_x,
    flux_y,
    send_y,
    send_z,
    halo_x,
    halo_y,
    halo_z,
    result,
    choose,
    row_choice,
    spread,
    row_send,
    row_recv,
    column_send,
    column_recv,
    plane_send,
    plane_recv,
    load_sem,
    store_sem,
    halo_send_sem,
    halo_recv_sem,
    row_send_sem,
    row_recv_sem,
    column_send_sem,
    column_recv_sem,
    plane_send_sem,
    plane_recv_sem,
):
    n_gx, n_gy, n_gz = sizes
    gx, gy, gz = (lax.axis_index(axis) for axis in AXES)
    half = lax.rem(gx, 2)
    plane = lax.div(gx, 2)
    n_plane = n_gx // 2
    n_row = 2 * n_gy
    my_row = half * n_gy + gy

    def row_device(t):
        return (plane * 2 + lax.div(t, n_gy), lax.rem(t, n_gy), gz)

    def column_device(t):
        return (gx, gy, t)

    def plane_device(t):
        return (t * 2 + half, gy, gz)

    barrier = pltpu.get_barrier_semaphore()
    me = (gx, gy, gz)
    ups, downs, has_up, has_down = [], [], [], []
    for d in range(3):
        up, down = list(me), list(me)
        up[d] = jnp.minimum(me[d] + 1, sizes[d] - 1)
        down[d] = jnp.maximum(me[d] - 1, 0)
        ups.append(tuple(up))
        downs.append(tuple(down))
        has_up.append(me[d] < sizes[d] - 1)
        has_down.append(me[d] > 0)

    def greet(to):
        pl.semaphore_signal(barrier, inc=1, device_id=to, device_id_type=MESH)

    cross_up = jnp.logical_and(half == 1, has_up[0])
    cross_down = jnp.logical_and(half == 0, has_down[0])
    for has, to in ((cross_up, ups[0]), (cross_down, downs[0])):

        @pl.when(has)
        def _(to=to):
            greet(to)

    greeted = []
    for n, mine, device, near in (
        (n_row, my_row, row_device, (1, n_row - 1, n_row // 2)),
        (n_gz, gz, column_device, (1, n_gz - 1)),
    ):
        for r in near:
            greet(device(lax.rem(mine + r, n)))
        greeted.append(near)

    loads = []
    for i, (src, dst) in enumerate(
        (
            (density_hbm, density),
            (velocity_hbm, velocity),
            (stiffness_hbm, stiffness),
            (sponge_hbm, sponge),
            (adjoint_hbm, fields.at[0]),
            (source_hbm, source),
        )
    ):
        copy = pltpu.make_async_copy(src, dst, load_sem.at[i])
        copy.start()
        loads.append(copy)

    for n, mine, device, near in (
        (n_row, my_row, row_device, greeted[0]),
        (n_gz, gz, column_device, greeted[1]),
        (n_plane, plane, plane_device, ()),
    ):
        for r in range(1, n):
            if r not in near:
                greet(device(lax.rem(mine + r, n)))
    expected = (
        jnp.int32(n_row - 1 + n_gz - 1 + n_plane - 1)
        + jnp.where(cross_up, 1, 0)
        + jnp.where(cross_down, 1, 0)
    )

    for d, halo in enumerate((halo_x, halo_y, halo_z)):
        for side, has in ((0, has_down[d]), (1, has_up[d])):

            @pl.when(jnp.logical_not(has))
            def _(halo=halo, side=side):
                for k in range(STAGES):
                    halo[k, side] = jnp.zeros(halo.shape[2:], jnp.float32)

    level = level_ref[gy, gz, gx]
    scale = 0.5 * step_length * lax.shift_left(jnp.int32(1), level).astype(jnp.float32)
    for copy in loads[:4]:
        copy.wait()
    for x in range(X):
        rho = density[x]
        speed[:, x] = scale * velocity[:, x]
        pull[x] = scale * rho
        push[x] = scale * stiffness[x]
        inverse[x] = scale / rho
        damp[x] = 1.0 - step_length * sponge[x]
    loads[4].wait()

    sub = lax.broadcasted_iota(jnp.int32, (Y, Z), 0)
    lane = lax.broadcasted_iota(jnp.int32, (Y, Z), 1)
    first_y, last_y = sub == 0, sub == Y - 1
    first_z, last_z = lane == 0, lane == Z - 1

    def flux(v, joint, x, d):
        c = speed[d, x]
        q = [c * v[f] for f in range(F)]
        q[1 + d] = q[1 + d] + joint
        q[4] = q[4] + inverse[x] * v[1 + d]
        return q

    def joint_term(v, x):
        return pull[x] * v[0] + push[x] * v[4]

    def halo_copy(k, d, side):
        parts = pl.ds(0, F + 1 if k == 0 else F)
        if d == 0:
            src, dst = flux_x.at[k, (X - 1) * side, parts], halo_x.at[k, 1 - side, parts]
        elif d == 1:
            src, dst = send_y.at[k, side, parts], halo_y.at[k, 1 - side, parts]
        else:
            src, dst = send_z.at[k, side], halo_z.at[k, 1 - side]
        return pltpu.make_async_remote_copy(
            src_ref=src,
            dst_ref=dst,
            send_sem=halo_send_sem.at[k, d, side],
            recv_sem=halo_recv_sem.at[k, d, 1 - side],
            device_id=ups[d] if side else downs[d],
            device_id_type=MESH,
        )

    def send_halo(k, d):
        for side, has in ((1, has_up[d]), (0, has_down[d])):

            @pl.when(has)
            def _(side=side):
                halo_copy(k, d, side).start()

    def wait_halo(k, d):
        for side, has in ((1, has_down[d]), (0, has_up[d])):

            @pl.when(has)
            def _(side=side):
                halo_copy(k, d, side).wait_recv()

    def finish_halo(k, add):
        wait_halo(k, 1)
        wait_halo(k, 2)
        low_z, high_z = halo_z[k, 0], halo_z[k, 1]
        for f in range(F):
            low_y, high_y = halo_y[k, 0, f], halo_y[k, 1, f]
            for x in range(X):
                at = f * X + x
                delta = jnp.where(
                    last_y,
                    jnp.broadcast_to(high_y[x : x + 1], (Y, Z)),
                    jnp.where(first_y, -jnp.broadcast_to(low_y[x : x + 1], (Y, Z)), 0.0),
                )
                delta += jnp.where(
                    last_z,
                    jnp.broadcast_to(high_z[:, at : at + 1], (Y, Z)),
                    jnp.where(first_z, -jnp.broadcast_to(low_z[:, at : at + 1], (Y, Z)), 0.0),
                )
                add(f, x, delta)
        wait_halo(k, 0)
        for f in range(F):
            add(f, 0, -halo_x[k, 0, f])
            add(f, X - 1, halo_x[k, 1, f])

    def owner_of(i, j, k):
        return owner_ref[patch_ref[j, k, i]]

    def row_of(o):
        ox = lax.div(o, n_gy * n_gz)
        return lax.rem(ox, 2) * n_gy + lax.rem(lax.div(o, n_gz), n_gy)

    def cell_of(o):
        return lax.rem(o, n_gz) * n_plane + lax.div(o, 2 * n_gy * n_gz)

    row_index = lax.broadcasted_iota(jnp.int32, (TILE, Z), 0)

    def route_tables():
        owners = {}

        def owner(di, j, dk):
            if (di, j, dk) not in owners:
                i = jnp.clip(plane * 2 + di, 0, n_gx - 1)
                owners[di, j, dk] = owner_of(i, j, jnp.clip(gz + dk, 0, n_gz - 1))
            return owners[di, j, dk]

        lanes = lax.broadcasted_iota(jnp.int32, (1, n_row * TILE), 1)
        target = jnp.full((1, n_row * TILE), -1, jnp.int32)
        for t in range(n_row):
            di, j = t // n_gy, t % n_gy
            bricks = [(0, di, j, 0, None)]
            bricks.append((1, di + 1, j, 0, plane < n_plane - 1 if di == 1 else None))
            bricks.append((2, di - 1, j, 0, plane > 0 if di == 0 else None))
            if j < n_gy - 1:
                bricks.append((3, di, j + 1, 0, None))
            if j > 0:
                bricks.append((4, di, j - 1, 0, None))
            bricks.append((5, di, j, 1, has_up[2]))
            bricks.append((6, di, j, -1, has_down[2]))
            for r, bi, bj, bk, there in bricks:
                cell = cell_of(owner(bi, bj, bk))
                if there is not None:
                    cell = jnp.where(there, cell, -1)
                target = jnp.where(lanes == t * TILE + r, cell, target)
        choose[...] = (
            lax.broadcasted_iota(jnp.int32, (n_plane * n_gz, n_row * TILE), 0) == target
        ).astype(jnp.float32)
        to_row = jnp.full((TILE, Z), -1, jnp.int32)
        places = [(me, None)]
        for d in range(3):
            places += [(ups[d], has_up[d]), (downs[d], has_down[d])]
        for r, (place, there) in enumerate(places):
            row = row_of(owner_of(*place))
            if there is not None:
                row = jnp.where(there, row, -1)
            to_row = jnp.where(row_index == r, row, to_row)
        row_choice[...] = to_row
        spread_to = lax.broadcasted_iota(jnp.int32, (Z, Z), 1)
        spread[...] = (
            lax.broadcasted_iota(jnp.int32, (Z, Z), 0)
            == BZ * lax.rem(spread_to, BOXES) + lax.div(spread_to, BOXES)
        ).astype(jnp.float32)

    loads[5].wait()
    for side in range(2):
        flux_x[0, (X - 1) * side, F] = source[(X - 1) * side]

    for k in range(STAGES):
        for x in (0, X - 1):
            v = [fields[k, f, x] for f in range(F)]
            q = flux(v, joint_term(v, x), x, 0)
            for f in range(F):
                flux_x[k, x, f] = q[f]
        if k == 0:
            pl.semaphore_wait(barrier, expected)
        send_halo(k, 0)
        packs = [jnp.zeros((Y, Z), jnp.float32), jnp.zeros((Y, Z), jnp.float32)]
        for x in range(X):
            v = [fields[k, f, x] for f in range(F)]
            joint = joint_term(v, x)
            if 0 < x < X - 1:
                q = flux(v, joint, x, 0)
                for f in range(F):
                    flux_x[k, x, f] = q[f]
            q = flux(v, joint, x, 2)
            columns = q + [source[x]] if k == 0 else q
            for f, column in enumerate(columns):
                here = lane == f * X + x
                packs[0] = jnp.where(here, jnp.broadcast_to(column[:, 0:1], (Y, Z)), packs[0])
                packs[1] = jnp.where(here, jnp.broadcast_to(column[:, Z - 1 : Z], (Y, Z)), packs[1])
            for f in range(F):
                fields[k + 1, f, x] = (
                    damp[x] * v[f]
                    + jnp.where(last_z, 0.0, pltpu.roll(q[f], Z - 1, 1))
                    - jnp.where(first_z, 0.0, pltpu.roll(q[f], 1, 1))
                )
            q = flux(v, joint, x, 1)
            if k == 0:
                flux_y[k, F, pl.ds(x * Y, Y), :] = source[x]
            for f in range(F):
                flux_y[k, f, pl.ds(x * Y, Y), :] = q[f]
                fields[k + 1, f, x] += jnp.where(last_y, 0.0, pltpu.roll(q[f], Y - 1, 0)) - jnp.where(
                    first_y, 0.0, pltpu.roll(q[f], 1, 0)
                )
        for side in range(2):
            send_z[k, side] = packs[side]
        send_halo(k, 2)
        for f in range(F + 1 if k == 0 else F):
            for side in range(2):
                send_y[k, side, f] = flux_y[k, f, pl.ds((Y - 1) * side, X, stride=Y), :]
        send_halo(k, 1)
        for x in range(X):
            for f in range(F):
                if x == 0:
                    fields[k + 1, f, x] += flux_x[k, x + 1, f]
                elif x == X - 1:
                    fields[k + 1, f, x] -= flux_x[k, x - 1, f]
                else:
                    fields[k + 1, f, x] += flux_x[k, x + 1, f] - flux_x[k, x - 1, f]
        if k == 0:
            route_tables()
        if k < STAGES - 1:

            def add(f, x, delta):
                fields[k + 1, f, x] += delta

            finish_halo(k, add)

    sixth = 0.5 * third
    tiles = []
    for f in range(F):
        total = jnp.zeros((Y, Z), jnp.float32)
        for x in range(X):
            value = third * fields[0, f, x] + 0.5 * fields[1, f, x] + sixth * fields[STAGES, f, x]
            result[f, x] = value
            total += value * source[x]
        weighted = [
            total,
            -sixth * flux_x[STAGES - 1, X - 1, f] * halo_x[0, 1, F],
            sixth * flux_x[STAGES - 1, 0, f] * halo_x[0, 0, F],
            -sixth * send_y[STAGES - 1, 1, f] * halo_y[0, 1, F],
            sixth * send_y[STAGES - 1, 0, f] * halo_y[0, 0, F],
        ]
        tile = jnp.zeros((TILE, Z), jnp.float32)
        for r, product in enumerate(weighted):
            line = jnp.sum(product, axis=0, keepdims=True)
            tile = jnp.where(row_index == r, jnp.broadcast_to(line, (TILE, Z)), tile)
        tiles.append(tile)

    block = jnp.zeros((TILE, Z), jnp.float32)
    for f in range(F):
        tile = tiles[f]
        for shift in (1, 2, 4, 8):
            tile = tile + pltpu.roll(tile, Z - shift, 1)
        if f:
            tile = pltpu.roll(tile, f, 1)
        block = jnp.where(lax.rem(lane, BZ) == f, tile, block)
    for side, row, sign in ((1, 5, -sixth), (0, 6, sixth)):
        shape = halo_z[0, side]
        shapes = jnp.zeros((Y, Z), jnp.float32)
        for f in range(F):
            moved = pltpu.roll(shape, Z - (F - f) * X, 1)
            shapes = jnp.where(lax.div(lane, X) == f, moved, shapes)
        line = jnp.broadcast_to(
            jnp.sum(sign * send_z[STAGES - 1, side] * shapes, axis=0, keepdims=True), (TILE, Z)
        )
        for shift in (1, 2, 4):
            line = line + pltpu.roll(line, Z - shift, 1)
        box = 0 if side else Z - BZ
        for f in range(F):
            moved = pltpu.roll(line, (box + f - f * X) % Z, 1)
            block = jnp.where(jnp.logical_and(row_index == row, lane == box + f), moved, block)
    block = step_length * block

    to_row = row_choice[...]
    for t in range(n_row):
        row_send[t] = jnp.where(to_row == t, block, 0.0)

    def ring_copy(n, mine, device, src, dst, sems, r):
        t = lax.rem(mine + r, n)
        return pltpu.make_async_remote_copy(
            src_ref=src.at[t],
            dst_ref=dst.at[mine],
            send_sem=sems[0].at[r],
            recv_sem=sems[1].at[r],
            device_id=device(t),
            device_id_type=MESH,
        )

    row_copy = functools.partial(
        ring_copy, n_row, my_row, row_device, row_send, row_recv, (row_send_sem, row_recv_sem)
    )
    column_copy = functools.partial(
        ring_copy, n_gz, gz, column_device, column_send, column_recv, (column_send_sem, column_recv_sem)
    )
    plane_copy = functools.partial(
        ring_copy, n_plane, plane, plane_device, plane_send, plane_recv, (plane_send_sem, plane_recv_sem)
    )

    def far_first(n):
        return sorted(range(1, n), key=lambda r: -min(r, n - r))

    for r in far_first(n_row):
        row_copy(r).start()
    row_recv[my_row] = row_send[my_row]
    for r in range(1, n_row):
        row_copy(r).wait_recv()
    rows = row_recv[...].reshape(n_row * TILE, Z)
    cells = jnp.dot(
        choose[...], rows, preferred_element_type=jnp.float32, precision=lax.Precision.HIGHEST
    )
    for t in range(n_gz):
        column_send[t] = cells[t * n_plane : (t + 1) * n_plane]
    for r in far_first(n_gz):
        column_copy(r).start()
    column_recv[gz] = column_send[gz]

    def add_result(f, x, delta):
        result[f, x] += sixth * delta

    finish_halo(STAGES - 1, add_result)
    store = pltpu.make_async_copy(result, out_hbm, store_sem)
    store.start()

    for r in range(1, n_gz):
        column_copy(r).wait_recv()
    planes = column_recv[0]
    for t in range(1, n_gz):
        planes += column_recv[t]
    for t in range(n_plane):
        plane_send[t] = planes[t : t + 1]
    for r in far_first(n_plane):
        plane_copy(r).start()
    plane_recv[plane] = plane_send[plane]
    for k in range(STAGES):
        for d in range(3):
            for side, has in ((1, has_up[d]), (0, has_down[d])):

                @pl.when(has)
                def _(side=side, k=k, d=d):
                    halo_copy(k, d, side).wait_send()

    for r in range(1, n_row):
        row_copy(r).wait_send()
    for r in range(1, n_gz):
        column_copy(r).wait_send()
    store.wait()
    for r in range(1, n_plane):
        plane_copy(r).wait_recv()
    own = plane_recv[0]
    for t in range(1, n_plane):
        own += plane_recv[t]
    ordered = jnp.dot(
        own, spread[...], preferred_element_type=jnp.float32, precision=lax.Precision.HIGHEST
    )
    grad_ref[...] = ordered[:, : F * BOXES]
    for r in range(1, n_plane):
        plane_copy(r).wait_send()


def solution(mesh):
    sizes = tuple(mesh.shape[axis] for axis in AXES)
    n_row = 2 * sizes[1]
    n_plane = sizes[0] // 2
    n_gz = sizes[2]

    def body(
        terminal_adjoint,
        density,
        velocity,
        stiffness,
        sponge,
        source_shape,
        brick_level,
        brick_patch,
        patch_owner,
    ):
        f32 = jnp.float32
        smem = pl.BlockSpec(memory_space=pltpu.SMEM)
        hbm = pl.BlockSpec(memory_space=pl.ANY)
        return pl.pallas_call(
            functools.partial(kernel, sizes),
            out_shape=(
                jax.ShapeDtypeStruct((F, X, Y, Z), f32),
                jax.ShapeDtypeStruct((1, F * BOXES), f32),
            ),
            in_specs=[smem] * 3 + [hbm] * 6,
            out_specs=(hbm, pl.BlockSpec(memory_space=pltpu.VMEM)),
            scratch_shapes=[
                pltpu.VMEM((STAGES + 1, F, X, Y, Z), f32),
                pltpu.VMEM((X, Y, Z), f32),
                pltpu.VMEM((3, X, Y, Z), f32),
                pltpu.VMEM((X, Y, Z), f32),
                pltpu.VMEM((X, Y, Z), f32),
                pltpu.VMEM((X, Y, Z), f32),
                pltpu.VMEM((3, X, Y, Z), f32),
                pltpu.VMEM((X, Y, Z), f32),
                pltpu.VMEM((X, Y, Z), f32),
                pltpu.VMEM((X, Y, Z), f32),
                pltpu.VMEM((X, Y, Z), f32),
                pltpu.VMEM((STAGES, X, F + 1, Y, Z), f32),
                pltpu.VMEM((STAGES, F + 1, X * Y, Z), f32),
                pltpu.VMEM((STAGES, 2, F + 1, X, Z), f32),
                pltpu.VMEM((STAGES, 2, Y, Z), f32),
                pltpu.VMEM((STAGES, 2, F + 1, Y, Z), f32),
                pltpu.VMEM((STAGES, 2, F + 1, X, Z), f32),
                pltpu.VMEM((STAGES, 2, Y, Z), f32),
                pltpu.VMEM((F, X, Y, Z), f32),
                pltpu.VMEM((n_plane * n_gz, n_row * TILE), f32),
                pltpu.VMEM((TILE, Z), jnp.int32),
                pltpu.VMEM((Z, Z), f32),
                pltpu.VMEM((n_row, TILE, Z), f32),
                pltpu.VMEM((n_row, TILE, Z), f32),
                pltpu.VMEM((n_gz, n_plane, Z), f32),
                pltpu.VMEM((n_gz, n_plane, Z), f32),
                pltpu.VMEM((n_plane, 1, Z), f32),
                pltpu.VMEM((n_plane, 1, Z), f32),
                pltpu.SemaphoreType.DMA((6,)),
                pltpu.SemaphoreType.DMA,
                pltpu.SemaphoreType.DMA((STAGES, 3, 2)),
                pltpu.SemaphoreType.DMA((STAGES, 3, 2)),
                pltpu.SemaphoreType.DMA((n_row,)),
                pltpu.SemaphoreType.DMA((n_row,)),
                pltpu.SemaphoreType.DMA((n_gz,)),
                pltpu.SemaphoreType.DMA((n_gz,)),
                pltpu.SemaphoreType.DMA((n_plane,)),
                pltpu.SemaphoreType.DMA((n_plane,)),
            ],
            compiler_params=pltpu.CompilerParams(collective_id=0, has_side_effects=True),
        )(
            jnp.transpose(brick_level, (1, 2, 0)),
            jnp.transpose(brick_patch, (1, 2, 0)),
            patch_owner,
            terminal_adjoint,
            density,
            velocity,
            stiffness,
            sponge,
            source_shape,
        )

    in_specs = (
        P(None, "gx", "gy", "gz"),
        P("gx", "gy", "gz"),
        P(None, "gx", "gy", "gz"),
        P("gx", "gy", "gz"),
        P("gx", "gy", "gz"),
        P("gx", "gy", "gz"),
        P(),
        P(),
        P(),
    )
    out_specs = (P(None, "gx", "gy", "gz"), P(AXES, None))
    return jax.shard_map(body, mesh=mesh, in_specs=in_specs, out_specs=out_specs, check_vma=False)
```

time: 62.2 us -> 55.9 us (0.90)
  Pallas kernels: 59.2 us -> 52.6 us
    pallas_call x1, Pallas kernels: 59.2 us -> 52.6 us  [body(): pl.pallas_call(functools.partial(kernel, sizes), out_shape=(jax.ShapeDtyp...]
where the time goes in v2:
time: 55.9 us; the launch traced here: 55.3 us
  Pallas kernels  52.6 us (94%)
  local copies, waits for them, and re-layouts  2.11 us (4%)
  between operations  0.65 us (1%)
    pallas_call x1, Pallas kernels, body(): pl.pallas_call(functools.partial(kernel, sizes), out_shape=(jax.ShapeDtyp...  52.6 us
    unnamed x4, local copies, waits for them, and re-layouts  2.11 us

profile of v2, /device:TPU:1, one launch (start us, length us, event | category | flops | bytes accessed | tf_op | source)
XLA Modules:
  0.0 55.3 jit_solution(9899755581624406941)
XLA Ops:
  0.6 52.6 %shard_map.104 = (f32[5,8,8,128]{3,2,1,0:T(8,128)}, f32[1,40]{1,0:T(1,128)}) custom-call(s32[8,8,16]{2,1,0:T(8,128)} %bitcast.2, s32[8,8,16]{2,1,0:T(8,128)} %bitcast.3, s32[1024]{0:T(1024)} %owner_ref.1, f32[5,8,8,128]{3,2,1,0:T(8,128)} %adjoint_hbm.1, f32[8,8,128]{2,1,0:T(8,128)} %density_hbm.1, f32[3,8,8,128]{3,2,1,0:T(8,128)} %velocity_hbm.1, ...), custom_call_target="tpu_custom_call" | custom-call | tf_op jit(solution)/shard_map/pallas_call | solution.py:520
  53.2 0.0 copy-start
  53.2 1.6 %copy.13 = f32[5,8,8,128]{3,2,1,0:T(8,128)} copy(f32[5,8,8,128]{3,2,1,0:T(8,128)} %get-tuple-element.4) | data formatting | bytes 327680
  54.8 0.0 copy-done
  54.8 0.5 copy.14
Async XLA Ops:
  53.2 1.6 %copy-start = (f32[1,40]{1,0:T(1,128)S(1)}, f32[1,40]{1,0:T(1,128)}, u32[]{:S(2)}) copy-start(f32[1,40]{1,0:T(1,128)} %get-tuple-element.5) | copy-start | bytes 484

commit v3 on v2

--- a/solution.py
+++ b/solution.py
@@ -23,17 +23,20 @@
 
 def kernel(
     sizes,
-    level_ref,
-    patch_ref,
-    owner_ref,
+    level_hbm,
+    patch_hbm,
+    owner_hbm,
     adjoint_hbm,
     density_hbm,
     velocity_hbm,
     stiffness_hbm,
     sponge_hbm,
     source_hbm,
-    out_hbm,
+    result,
     grad_ref,
+    level_ref,
+    patch_ref,
+    owner_ref,
     fields,
     density,
     velocity,
@@ -52,7 +55,6 @@
     halo_x,
     halo_y,
     halo_z,
-    result,
     choose,
     row_choice,
     spread,
@@ -63,7 +65,6 @@
     plane_send,
     plane_recv,
     load_sem,
-    store_sem,
     halo_send_sem,
     halo_recv_sem,
     row_send_sem,
@@ -72,6 +73,7 @@
     column_recv_sem,
     plane_send_sem,
     plane_recv_sem,
+    token_sem,
 ):
     n_gx, n_gy, n_gz = sizes
     gx, gy, gz = (lax.axis_index(axis) for axis in AXES)
@@ -113,14 +115,33 @@
         def _(to=to):
             greet(to)
 
-    greeted = []
-    for n, mine, device, near in (
-        (n_row, my_row, row_device, (1, n_row - 1, n_row // 2)),
+    rings = (
+        (n_row, my_row, row_device, (n_row // 2, 1, n_row - 1)),
         (n_gz, gz, column_device, (1, n_gz - 1)),
-    ):
+        (n_plane, plane, plane_device, (1, n_plane - 1)),
+    )
+    for n, mine, device, near in rings:
         for r in near:
             greet(device(lax.rem(mine + r, n)))
-        greeted.append(near)
+    expected = (
+        jnp.int32(sum(len(near) for _, _, _, near in rings))
+        + jnp.where(cross_up, 1, 0)
+        + jnp.where(cross_down, 1, 0)
+    )
+
+    def send_tokens(level):
+        for ring, (n, mine, device, _) in enumerate(rings):
+            for r in (level, n - level):
+                pl.semaphore_signal(
+                    token_sem.at[ring, level - 1],
+                    inc=1,
+                    device_id=device(lax.rem(mine + r, n)),
+                    device_id_type=MESH,
+                )
+
+    def wait_tokens(level):
+        for ring in range(len(rings)):
+            pl.semaphore_wait(token_sem.at[ring, level - 1], 2)
 
     loads = []
     for i, (src, dst) in enumerate(
@@ -131,26 +152,15 @@
             (sponge_hbm, sponge),
             (adjoint_hbm, fields.at[0]),
             (source_hbm, source),
+            (level_hbm, level_ref),
+            (patch_hbm, patch_ref),
+            (owner_hbm, owner_ref),
         )
     ):
         copy = pltpu.make_async_copy(src, dst, load_sem.at[i])
         copy.start()
         loads.append(copy)
 
-    for n, mine, device, near in (
-        (n_row, my_row, row_device, greeted[0]),
-        (n_gz, gz, column_device, greeted[1]),
-        (n_plane, plane, plane_device, ()),
-    ):
-        for r in range(1, n):
-            if r not in near:
-                greet(device(lax.rem(mine + r, n)))
-    expected = (
-        jnp.int32(n_row - 1 + n_gz - 1 + n_plane - 1)
-        + jnp.where(cross_up, 1, 0)
-        + jnp.where(cross_down, 1, 0)
-    )
-
     for d, halo in enumerate((halo_x, halo_y, halo_z)):
         for side, has in ((0, has_down[d]), (1, has_up[d])):
 
@@ -159,6 +169,7 @@
                 for k in range(STAGES):
                     halo[k, side] = jnp.zeros(halo.shape[2:], jnp.float32)
 
+    loads[6].wait()
     level = level_ref[gy, gz, gx]
     scale = 0.5 * step_length * lax.shift_left(jnp.int32(1), level).astype(jnp.float32)
     for copy in loads[:4]:
@@ -357,7 +368,12 @@
                 else:
                     fields[k + 1, f, x] += flux_x[k, x + 1, f] - flux_x[k, x - 1, f]
         if k == 0:
+            send_tokens(1)
+            loads[7].wait()
+            loads[8].wait()
             route_tables()
+            wait_tokens(1)
+            send_tokens(2)
         if k < STAGES - 1:
 
             def add(f, x, delta):
@@ -365,6 +381,7 @@
 
             finish_halo(k, add)
 
+    wait_tokens(2)
     sixth = 0.5 * third
     tiles = []
     for f in range(F):
@@ -458,8 +475,6 @@
         result[f, x] += sixth * delta
 
     finish_halo(STAGES - 1, add_result)
-    store = pltpu.make_async_copy(result, out_hbm, store_sem)
-    store.start()
 
     for r in range(1, n_gz):
         column_copy(r).wait_recv()
@@ -483,7 +498,6 @@
         row_copy(r).wait_send()
     for r in range(1, n_gz):
         column_copy(r).wait_send()
-    store.wait()
     for r in range(1, n_plane):
         plane_copy(r).wait_recv()
     own = plane_recv[0]
@@ -515,17 +529,19 @@
         patch_owner,
     ):
         f32 = jnp.float32
-        smem = pl.BlockSpec(memory_space=pltpu.SMEM)
         hbm = pl.BlockSpec(memory_space=pl.ANY)
         return pl.pallas_call(
             functools.partial(kernel, sizes),
             out_shape=(
-                jax.ShapeDtypeStruct((F, X, Y, Z), f32),
-                jax.ShapeDtypeStruct((1, F * BOXES), f32),
+                pltpu.VMEM((F, X, Y, Z), f32),
+                pltpu.VMEM((1, F * BOXES), f32),
             ),
-            in_specs=[smem] * 3 + [hbm] * 6,
-            out_specs=(hbm, pl.BlockSpec(memory_space=pltpu.VMEM)),
+            in_specs=[hbm] * 9,
+            out_specs=(pl.BlockSpec(memory_space=pltpu.VMEM),) * 2,
             scratch_shapes=[
+                pltpu.SMEM((sizes[1], sizes[2], sizes[0]), jnp.int32),
+                pltpu.SMEM((sizes[1], sizes[2], sizes[0]), jnp.int32),
+                pltpu.SMEM((sizes[0] * sizes[1] * sizes[2],), jnp.int32),
                 pltpu.VMEM((STAGES + 1, F, X, Y, Z), f32),
                 pltpu.VMEM((X, Y, Z), f32),
                 pltpu.VMEM((3, X, Y, Z), f32),
@@ -544,7 +560,6 @@
                 pltpu.VMEM((STAGES, 2, F + 1, Y, Z), f32),
                 pltpu.VMEM((STAGES, 2, F + 1, X, Z), f32),
                 pltpu.VMEM((STAGES, 2, Y, Z), f32),
-                pltpu.VMEM((F, X, Y, Z), f32),
                 pltpu.VMEM((n_plane * n_gz, n_row * TILE), f32),
                 pltpu.VMEM((TILE, Z), jnp.int32),
                 pltpu.VMEM((Z, Z), f32),
@@ -554,8 +569,7 @@
                 pltpu.VMEM((n_gz, n_plane, Z), f32),
                 pltpu.VMEM((n_plane, 1, Z), f32),
                 pltpu.VMEM((n_plane, 1, Z), f32),
-                pltpu.SemaphoreType.DMA((6,)),
-                pltpu.SemaphoreType.DMA,
+                pltpu.SemaphoreType.DMA((9,)),
                 pltpu.SemaphoreType.DMA((STAGES, 3, 2)),
                 pltpu.SemaphoreType.DMA((STAGES, 3, 2)),
                 pltpu.SemaphoreType.DMA((n_row,)),
@@ -564,6 +578,7 @@
                 pltpu.SemaphoreType.DMA((n_gz,)),
                 pltpu.SemaphoreType.DMA((n_plane,)),
                 pltpu.SemaphoreType.DMA((n_plane,)),
+                pltpu.SemaphoreType.REGULAR((3, 2)),
             ],
             compiler_params=pltpu.CompilerParams(collective_id=0, has_side_effects=True),
         )(

time: 55.9 us -> 50.7 us (0.907)
  Pallas kernels: 52.6 us -> 48 us
  local copies, waits for them, and re-layouts: 2.11 us -> 1.18 us
    pallas_call x1, Pallas kernels: 52.6 us -> 48 us  [body(): pl.pallas_call(functools.partial(kernel, sizes), out_shape=(pltpu.VMEM((F...]
    unnamed x4 -> x2, local copies, waits for them, and re-layouts: 2.11 us -> 1.18 us
where the time goes in v3:
time: 50.7 us; the launch traced here: 49.9 us
  Pallas kernels  48 us (95%)
  local copies, waits for them, and re-layouts  1.18 us (2%)
  between operations  0.64 us (1%)
    pallas_call x1, Pallas kernels, body(): pl.pallas_call(functools.partial(kernel, sizes), out_shape=(pltpu.VMEM((F...  48 us
    unnamed x2, local copies, waits for them, and re-layouts  1.18 us

profile of v3, /device:TPU:1, one launch (start us, length us, event | category | flops | bytes accessed | tf_op | source)
XLA Modules:
  0.0 49.9 jit_solution(10711700649253507967)
XLA Ops:
  0.6 48.0 %shard_map.104 = (f32[5,8,8,128]{3,2,1,0:T(8,128)S(1)}, f32[1,40]{1,0:T(1,128)S(1)}) custom-call(s32[8,8,16]{2,1,0:T(8,128)} %bitcast.2, s32[8,8,16]{2,1,0:T(8,128)} %bitcast.3, s32[1024]{0:T(1024)} %owner_hbm.1, f32[5,8,8,128]{3,2,1,0:T(8,128)} %adjoint_hbm.1, f32[8,8,128]{2,1,0:T(8,128)} %density_hbm.1, f32[3,8,8,128]{3,2,1,0:T(8,128)} %velocity_hbm.1, ...), custom_call_target="tpu_custom_call" | custom-call | tf_op jit(solution)/shard_map/pallas_call | solution.py:533
  48.7 0.7 %copy.13 = f32[5,8,8,128]{3,2,1,0:T(8,128)} copy(f32[5,8,8,128]{3,2,1,0:T(8,128)S(1)} %get-tuple-element.2) | data formatting | bytes 327680
  49.4 0.5 %copy.14 = f32[1,40]{1,0:T(1,128)} copy(f32[1,40]{1,0:T(1,128)S(1)} %get-tuple-element.3) | data formatting | bytes 320

commit v4 on v3

--- a/solution.py
+++ b/solution.py
@@ -15,6 +15,8 @@
 BZ = 16
 BOXES = Z // BZ
 TILE = 8
+ROWS = TILE // 2
+LAYERS = 5
 STAGES = 3
 step_length = 0.14
 third = 1.0 / 3.0
@@ -55,25 +57,27 @@
     halo_x,
     halo_y,
     halo_z,
+    send_x,
+    layers,
+    halo_layers,
     choose,
     row_choice,
     spread,
     row_send,
     row_recv,
-    column_send,
-    column_recv,
-    plane_send,
-    plane_recv,
+    cell_send,
+    cell_recv,
     load_sem,
     halo_send_sem,
     halo_recv_sem,
+    layer_send_sem,
+    layer_recv_sem,
     row_send_sem,
     row_recv_sem,
-    column_send_sem,
-    column_recv_sem,
-    plane_send_sem,
-    plane_recv_sem,
+    cell_send_sem,
+    cell_recv_sem,
     token_sem,
+    line_sem,
 ):
     n_gx, n_gy, n_gz = sizes
     gx, gy, gz = (lax.axis_index(axis) for axis in AXES)
@@ -82,6 +86,7 @@
     n_plane = n_gx // 2
     n_row = 2 * n_gy
     my_row = half * n_gy + gy
+    my_cell = gz * n_plane + plane
 
     def row_device(t):
         return (plane * 2 + lax.div(t, n_gy), lax.rem(t, n_gy), gz)
@@ -91,6 +96,12 @@
 
     def plane_device(t):
         return (t * 2 + half, gy, gz)
+
+    def cell_device(dz, dy):
+        return (lax.rem(plane + dz, n_plane) * 2 + half, gy, lax.rem(gz + dy, n_gz))
+
+    def cell_row(dz, dy):
+        return lax.rem(gz + dy, n_gz) * n_plane + lax.rem(plane + dz, n_plane)
 
     barrier = pltpu.get_barrier_semaphore()
     me = (gx, gy, gz)
@@ -103,45 +114,6 @@
         downs.append(tuple(down))
         has_up.append(me[d] < sizes[d] - 1)
         has_down.append(me[d] > 0)
-
-    def greet(to):
-        pl.semaphore_signal(barrier, inc=1, device_id=to, device_id_type=MESH)
-
-    cross_up = jnp.logical_and(half == 1, has_up[0])
-    cross_down = jnp.logical_and(half == 0, has_down[0])
-    for has, to in ((cross_up, ups[0]), (cross_down, downs[0])):
-
-        @pl.when(has)
-        def _(to=to):
-            greet(to)
-
-    rings = (
-        (n_row, my_row, row_device, (n_row // 2, 1, n_row - 1)),
-        (n_gz, gz, column_device, (1, n_gz - 1)),
-        (n_plane, plane, plane_device, (1, n_plane - 1)),
-    )
-    for n, mine, device, near in rings:
-        for r in near:
-            greet(device(lax.rem(mine + r, n)))
-    expected = (
-        jnp.int32(sum(len(near) for _, _, _, near in rings))
-        + jnp.where(cross_up, 1, 0)
-        + jnp.where(cross_down, 1, 0)
-    )
-
-    def send_tokens(level):
-        for ring, (n, mine, device, _) in enumerate(rings):
-            for r in (level, n - level):
-                pl.semaphore_signal(
-                    token_sem.at[ring, level - 1],
-                    inc=1,
-                    device_id=device(lax.rem(mine + r, n)),
-                    device_id_type=MESH,
-                )
-
-    def wait_tokens(level):
-        for ring in range(len(rings)):
-            pl.semaphore_wait(token_sem.at[ring, level - 1], 2)
 
     loads = []
     for i, (src, dst) in enumerate(
@@ -161,6 +133,74 @@
         copy.start()
         loads.append(copy)
 
+    def greet(to):
+        pl.semaphore_signal(barrier, inc=1, device_id=to, device_id_type=MESH)
+
+    cross_up = jnp.logical_and(half == 1, has_up[0])
+    cross_down = jnp.logical_and(half == 0, has_down[0])
+    for has, to in ((cross_up, ups[0]), (cross_down, downs[0])):
+
+        @pl.when(has)
+        def _(to=to):
+            greet(to)
+
+    rings = (
+        (n_row, my_row, row_device, (n_row // 2, 1, n_row - 1)),
+        (n_gz, gz, column_device, (1, n_gz - 1)),
+    )
+    for n, mine, device, near in rings:
+        for r in near:
+            greet(device(lax.rem(mine + r, n)))
+
+    def planes_at(step):
+        up, down = plane + step, plane - step
+        return (
+            (up < n_plane, plane_device(jnp.minimum(up, n_plane - 1))),
+            (down >= 0, plane_device(jnp.maximum(down, 0))),
+        )
+
+    def line_count(step):
+        return sum(jnp.where(has, 1, 0) for has, _ in planes_at(step))
+
+    for has, to in planes_at(1):
+
+        @pl.when(has)
+        def _(to=to):
+            greet(to)
+
+    expected = (
+        jnp.int32(sum(len(near) for _, _, _, near in rings))
+        + line_count(1)
+        + jnp.where(cross_up, 1, 0)
+        + jnp.where(cross_down, 1, 0)
+    )
+
+    def send_tokens(level):
+        for ring, (n, mine, device, _) in enumerate(rings):
+            for r in (level, n - level):
+                pl.semaphore_signal(
+                    token_sem.at[ring, level - 1],
+                    inc=1,
+                    device_id=device(lax.rem(mine + r, n)),
+                    device_id_type=MESH,
+                )
+
+    def wait_tokens(level):
+        for ring in range(len(rings)):
+            pl.semaphore_wait(token_sem.at[ring, level - 1], 2)
+
+    def send_line(level):
+        for has, to in planes_at(1 << level):
+
+            @pl.when(has)
+            def _(to=to):
+                pl.semaphore_signal(
+                    line_sem.at[level], inc=1, device_id=to, device_id_type=MESH
+                )
+
+    def wait_line(level):
+        pl.semaphore_wait(line_sem.at[level], line_count(1 << level))
+
     for d, halo in enumerate((halo_x, halo_y, halo_z)):
         for side, has in ((0, has_down[d]), (1, has_up[d])):
 
@@ -168,6 +208,8 @@
             def _(halo=halo, side=side):
                 for k in range(STAGES):
                     halo[k, side] = jnp.zeros(halo.shape[2:], jnp.float32)
+                if halo is halo_x:
+                    halo_layers[side] = jnp.zeros(halo_layers.shape[1:], jnp.float32)
 
     loads[6].wait()
     level = level_ref[gy, gz, gx]
@@ -201,7 +243,8 @@
     def halo_copy(k, d, side):
         parts = pl.ds(0, F + 1 if k == 0 else F)
         if d == 0:
-            src, dst = flux_x.at[k, (X - 1) * side, parts], halo_x.at[k, 1 - side, parts]
+            src = send_x.at[side] if k == 1 else flux_x.at[k, (X - 1) * side]
+            dst = halo_x.at[k, 1 - side]
         elif d == 1:
             src, dst = send_y.at[k, side, parts], halo_y.at[k, 1 - side, parts]
         else:
@@ -229,13 +272,47 @@
             def _(side=side):
                 halo_copy(k, d, side).wait_recv()
 
-    def finish_halo(k, add):
+    def layer_copy(side):
+        return pltpu.make_async_remote_copy(
+            src_ref=layers.at[side],
+            dst_ref=halo_layers.at[1 - side],
+            send_sem=layer_send_sem.at[side],
+            recv_sem=layer_recv_sem.at[1 - side],
+            device_id=ups[0] if side else downs[0],
+            device_id_type=MESH,
+        )
+
+    def each_side(act, up_first):
+        for side in (1, 0):
+            has = (has_up if (side == 1) == up_first else has_down)[0]
+
+            @pl.when(has)
+            def _(side=side):
+                act(layer_copy(side))
+
+    def send_outermost():
+        for side in range(2):
+            for f in range(F):
+                send_x[side, f] = fields[1, f, (X - 1) * side]
+        send_halo(1, 0)
+
+    def neighbour_flux(side):
+        at, sign = ((0, 1.0), (X - 1, -1.0))[side]
+        v = [halo_x[1, side, f] + sign * flux_x[0, at, f] for f in range(F)]
+        q = [halo_layers[side, 1] * v[f] for f in range(F)]
+        q[1] = q[1] + (halo_layers[side, 2] * v[0] + halo_layers[side, 3] * v[4])
+        q[4] = q[4] + halo_layers[side, 4] * v[1]
+        return q
+
+    def finish_halo(k, add, between=None):
         wait_halo(k, 1)
         wait_halo(k, 2)
         low_z, high_z = halo_z[k, 0], halo_z[k, 1]
-        for f in range(F):
-            low_y, high_y = halo_y[k, 0, f], halo_y[k, 1, f]
-            for x in range(X):
+        for x in (0, X - 1, *range(1, X - 1)):
+            if k == 0 and x == 1:
+                send_outermost()
+            for f in range(F):
+                low_y, high_y = halo_y[k, 0, f], halo_y[k, 1, f]
                 at = f * X + x
                 delta = jnp.where(
                     last_y,
@@ -248,10 +325,17 @@
                     jnp.where(first_z, -jnp.broadcast_to(low_z[:, at : at + 1], (Y, Z)), 0.0),
                 )
                 add(f, x, delta)
+        if between is not None:
+            between()
         wait_halo(k, 0)
+        if k == 1:
+            each_side(lambda copy: copy.wait_recv(), False)
+            low, high = neighbour_flux(0), neighbour_flux(1)
+        else:
+            low, high = ([halo_x[k, side, f] for f in range(F)] for side in range(2))
         for f in range(F):
-            add(f, 0, -halo_x[k, 0, f])
-            add(f, X - 1, halo_x[k, 1, f])
+            add(f, 0, -low[f])
+            add(f, X - 1, high[f])
 
     def owner_of(i, j, k):
         return owner_ref[patch_ref[j, k, i]]
@@ -264,6 +348,8 @@
         return lax.rem(o, n_gz) * n_plane + lax.div(o, 2 * n_gy * n_gz)
 
     row_index = lax.broadcasted_iota(jnp.int32, (TILE, Z), 0)
+    packed_row = lax.broadcasted_iota(jnp.int32, (ROWS, Z), 0)
+    packed_half = lax.rem(lax.broadcasted_iota(jnp.int32, (ROWS, Z), 1), BZ) // (BZ // 2)
 
     def route_tables():
         owners = {}
@@ -274,8 +360,8 @@
                 owners[di, j, dk] = owner_of(i, j, jnp.clip(gz + dk, 0, n_gz - 1))
             return owners[di, j, dk]
 
-        lanes = lax.broadcasted_iota(jnp.int32, (1, n_row * TILE), 1)
-        target = jnp.full((1, n_row * TILE), -1, jnp.int32)
+        lanes = lax.broadcasted_iota(jnp.int32, (1, n_row * ROWS), 1)
+        targets = [jnp.full((1, n_row * ROWS), -1, jnp.int32) for _ in range(2)]
         for t in range(n_row):
             di, j = t // n_gy, t % n_gy
             bricks = [(0, di, j, 0, None)]
@@ -288,14 +374,15 @@
             bricks.append((5, di, j, 1, has_up[2]))
             bricks.append((6, di, j, -1, has_down[2]))
             for r, bi, bj, bk, there in bricks:
-                cell = cell_of(owner(bi, bj, bk))
+                cell = cell_of(owner(bi, bj, bk)) + r // ROWS * n_plane * n_gz
                 if there is not None:
                     cell = jnp.where(there, cell, -1)
-                target = jnp.where(lanes == t * TILE + r, cell, target)
-        choose[...] = (
-            lax.broadcasted_iota(jnp.int32, (n_plane * n_gz, n_row * TILE), 0) == target
-        ).astype(jnp.float32)
-        to_row = jnp.full((TILE, Z), -1, jnp.int32)
+                at = t * ROWS + r % ROWS
+                targets[r // ROWS] = jnp.where(lanes == at, cell, targets[r // ROWS])
+        cells = lax.broadcasted_iota(jnp.int32, (2 * n_plane * n_gz, n_row * ROWS), 0)
+        choose[...] = jnp.logical_or(cells == targets[0], cells == targets[1]).astype(jnp.float32)
+        to_row = jnp.full((ROWS, Z), -1, jnp.int32)
+        slots = packed_row + ROWS * packed_half
         places = [(me, None)]
         for d in range(3):
             places += [(ups[d], has_up[d]), (downs[d], has_down[d])]
@@ -303,7 +390,7 @@
             row = row_of(owner_of(*place))
             if there is not None:
                 row = jnp.where(there, row, -1)
-            to_row = jnp.where(row_index == r, row, to_row)
+            to_row = jnp.where(slots == r, row, to_row)
         row_choice[...] = to_row
         spread_to = lax.broadcasted_iota(jnp.int32, (Z, Z), 1)
         spread[...] = (
@@ -313,7 +400,9 @@
 
     loads[5].wait()
     for side in range(2):
-        flux_x[0, (X - 1) * side, F] = source[(X - 1) * side]
+        x = (X - 1) * side
+        for i, layer in enumerate((source[x], speed[0, x], pull[x], push[x], inverse[x])):
+            layers[side, i] = layer
 
     for k in range(STAGES):
         for x in (0, X - 1):
@@ -323,7 +412,8 @@
                 flux_x[k, x, f] = q[f]
         if k == 0:
             pl.semaphore_wait(barrier, expected)
-        send_halo(k, 0)
+        if k != 1:
+            send_halo(k, 0)
         packs = [jnp.zeros((Y, Z), jnp.float32), jnp.zeros((Y, Z), jnp.float32)]
         for x in range(X):
             v = [fields[k, f, x] for f in range(F)]
@@ -368,6 +458,7 @@
                 else:
                     fields[k + 1, f, x] += flux_x[k, x + 1, f] - flux_x[k, x - 1, f]
         if k == 0:
+            each_side(lambda copy: copy.start(), True)
             send_tokens(1)
             loads[7].wait()
             loads[8].wait()
@@ -379,9 +470,15 @@
             def add(f, x, delta):
                 fields[k + 1, f, x] += delta
 
-            finish_halo(k, add)
-
-    wait_tokens(2)
+            def pass_line():
+                wait_line(0)
+                send_line(1)
+
+            if k == 1:
+                wait_tokens(2)
+                send_line(0)
+            finish_halo(k, add, pass_line if k == 1 else None)
+
     sixth = 0.5 * third
     tiles = []
     for f in range(F):
@@ -392,8 +489,8 @@
             total += value * source[x]
         weighted = [
             total,
-            -sixth * flux_x[STAGES - 1, X - 1, f] * halo_x[0, 1, F],
-            sixth * flux_x[STAGES - 1, 0, f] * halo_x[0, 0, F],
+            -sixth * flux_x[STAGES - 1, X - 1, f] * halo_layers[1, 0],
+            sixth * flux_x[STAGES - 1, 0, f] * halo_layers[0, 0],
             -sixth * send_y[STAGES - 1, 1, f] * halo_y[0, 1, F],
             sixth * send_y[STAGES - 1, 0, f] * halo_y[0, 0, F],
         ]
@@ -428,6 +525,7 @@
             block = jnp.where(jnp.logical_and(row_index == row, lane == box + f), moved, block)
     block = step_length * block
 
+    block = jnp.where(packed_half == 0, block[:ROWS], pltpu.roll(block, BZ // 2, 1)[ROWS:])
     to_row = row_choice[...]
     for t in range(n_row):
         row_send[t] = jnp.where(to_row == t, block, 0.0)
@@ -446,12 +544,16 @@
     row_copy = functools.partial(
         ring_copy, n_row, my_row, row_device, row_send, row_recv, (row_send_sem, row_recv_sem)
     )
-    column_copy = functools.partial(
-        ring_copy, n_gz, gz, column_device, column_send, column_recv, (column_send_sem, column_recv_sem)
-    )
-    plane_copy = functools.partial(
-        ring_copy, n_plane, plane, plane_device, plane_send, plane_recv, (plane_send_sem, plane_recv_sem)
-    )
+
+    def cell_copy(dz, dy):
+        return pltpu.make_async_remote_copy(
+            src_ref=cell_send.at[cell_row(dz, dy)],
+            dst_ref=cell_recv.at[my_cell],
+            send_sem=cell_send_sem.at[dz * n_gz + dy],
+            recv_sem=cell_recv_sem.at[dz * n_gz + dy],
+            device_id=cell_device(dz, dy),
+            device_id_type=MESH,
+        )
 
     def far_first(n):
         return sorted(range(1, n), key=lambda r: -min(r, n - r))
@@ -459,33 +561,32 @@
     for r in far_first(n_row):
         row_copy(r).start()
     row_recv[my_row] = row_send[my_row]
+    wait_line(1)
+    send_line(2)
     for r in range(1, n_row):
         row_copy(r).wait_recv()
-    rows = row_recv[...].reshape(n_row * TILE, Z)
+    rows = jnp.concatenate([row_recv[t] for t in range(n_row)], axis=0)
     cells = jnp.dot(
         choose[...], rows, preferred_element_type=jnp.float32, precision=lax.Precision.HIGHEST
     )
-    for t in range(n_gz):
-        column_send[t] = cells[t * n_plane : (t + 1) * n_plane]
-    for r in far_first(n_gz):
-        column_copy(r).start()
-    column_recv[gz] = column_send[gz]
+    n_cell = n_gz * n_plane
+    first_half = lax.rem(lax.broadcasted_iota(jnp.int32, (n_cell, Z), 1), BZ) < BZ // 2
+    moved = jnp.where(first_half, 0.0, cells[n_cell:])
+    cells = jnp.where(first_half, cells[:n_cell], 0.0) + pltpu.roll(moved, Z - BZ // 2, 1)
+    for t in range(n_cell):
+        cell_send[t] = cells[t : t + 1]
+    wait_line(2)
+    hops = [0] + far_first(n_gz)
+    others = [(dz % n_plane, dy) for dz in range(1, n_plane + 1) for dy in hops]
+    others.remove((0, 0))
+    for dz, dy in others:
+        cell_copy(dz, dy).start()
+    cell_recv[my_cell] = cell_send[my_cell]
 
     def add_result(f, x, delta):
         result[f, x] += sixth * delta
 
     finish_halo(STAGES - 1, add_result)
-
-    for r in range(1, n_gz):
-        column_copy(r).wait_recv()
-    planes = column_recv[0]
-    for t in range(1, n_gz):
-        planes += column_recv[t]
-    for t in range(n_plane):
-        plane_send[t] = planes[t : t + 1]
-    for r in far_first(n_plane):
-        plane_copy(r).start()
-    plane_recv[plane] = plane_send[plane]
     for k in range(STAGES):
         for d in range(3):
             for side, has in ((1, has_up[d]), (0, has_down[d])):
@@ -494,21 +595,19 @@
                 def _(side=side, k=k, d=d):
                     halo_copy(k, d, side).wait_send()
 
+    each_side(lambda copy: copy.wait_send(), True)
+
     for r in range(1, n_row):
         row_copy(r).wait_send()
-    for r in range(1, n_gz):
-        column_copy(r).wait_send()
-    for r in range(1, n_plane):
-        plane_copy(r).wait_recv()
-    own = plane_recv[0]
-    for t in range(1, n_plane):
-        own += plane_recv[t]
+    for dz, dy in others:
+        cell_copy(dz, dy).wait_recv()
+    own = jnp.sum(cell_recv[...].reshape(n_gz * n_plane, Z), axis=0, keepdims=True)
     ordered = jnp.dot(
         own, spread[...], preferred_element_type=jnp.float32, precision=lax.Precision.HIGHEST
     )
     grad_ref[...] = ordered[:, : F * BOXES]
-    for r in range(1, n_plane):
-        plane_copy(r).wait_send()
+    for dz, dy in others:
+        cell_copy(dz, dy).wait_send()
 
 
 def solution(mesh):
@@ -553,32 +652,34 @@
                 pltpu.VMEM((X, Y, Z), f32),
                 pltpu.VMEM((X, Y, Z), f32),
                 pltpu.VMEM((X, Y, Z), f32),
-                pltpu.VMEM((STAGES, X, F + 1, Y, Z), f32),
+                pltpu.VMEM((STAGES, X, F, Y, Z), f32),
                 pltpu.VMEM((STAGES, F + 1, X * Y, Z), f32),
                 pltpu.VMEM((STAGES, 2, F + 1, X, Z), f32),
                 pltpu.VMEM((STAGES, 2, Y, Z), f32),
-                pltpu.VMEM((STAGES, 2, F + 1, Y, Z), f32),
+                pltpu.VMEM((STAGES, 2, F, Y, Z), f32),
                 pltpu.VMEM((STAGES, 2, F + 1, X, Z), f32),
                 pltpu.VMEM((STAGES, 2, Y, Z), f32),
-                pltpu.VMEM((n_plane * n_gz, n_row * TILE), f32),
-                pltpu.VMEM((TILE, Z), jnp.int32),
+                pltpu.VMEM((2, F, Y, Z), f32),
+                pltpu.VMEM((2, LAYERS, Y, Z), f32),
+                pltpu.VMEM((2, LAYERS, Y, Z), f32),
+                pltpu.VMEM((2 * n_plane * n_gz, n_row * ROWS), f32),
+                pltpu.VMEM((ROWS, Z), jnp.int32),
                 pltpu.VMEM((Z, Z), f32),
-                pltpu.VMEM((n_row, TILE, Z), f32),
-                pltpu.VMEM((n_row, TILE, Z), f32),
-                pltpu.VMEM((n_gz, n_plane, Z), f32),
-                pltpu.VMEM((n_gz, n_plane, Z), f32),
-                pltpu.VMEM((n_plane, 1, Z), f32),
-                pltpu.VMEM((n_plane, 1, Z), f32),
+                pltpu.VMEM((n_row, ROWS, Z), f32),
+                pltpu.VMEM((n_row, ROWS, Z), f32),
+                pltpu.VMEM((n_plane * n_gz, 1, Z), f32),
+                pltpu.VMEM((n_plane * n_gz, 1, Z), f32),
                 pltpu.SemaphoreType.DMA((9,)),
                 pltpu.SemaphoreType.DMA((STAGES, 3, 2)),
                 pltpu.SemaphoreType.DMA((STAGES, 3, 2)),
+                pltpu.SemaphoreType.DMA((2,)),
+                pltpu.SemaphoreType.DMA((2,)),
                 pltpu.SemaphoreType.DMA((n_row,)),
                 pltpu.SemaphoreType.DMA((n_row,)),
-                pltpu.SemaphoreType.DMA((n_gz,)),
-                pltpu.SemaphoreType.DMA((n_gz,)),
-                pltpu.SemaphoreType.DMA((n_plane,)),
-                pltpu.SemaphoreType.DMA((n_plane,)),
-                pltpu.SemaphoreType.REGULAR((3, 2)),
+                pltpu.SemaphoreType.DMA((n_plane * n_gz,)),
+                pltpu.SemaphoreType.DMA((n_plane * n_gz,)),
+                pltpu.SemaphoreType.REGULAR((2, 2)),
+                pltpu.SemaphoreType.REGULAR((3,)),
             ],
             compiler_params=pltpu.CompilerParams(collective_id=0, has_side_effects=True),
         )(

time: 50.7 us -> 49.7 us (0.980); the launches traced: 49.9 us -> 49.5 us
  no operation moved by 1% of the time
where the time goes in v4:
time: 49.7 us; the launch traced here: 49.5 us
  Pallas kernels  47.6 us (96%)
  local copies, waits for them, and re-layouts  1.18 us (2%)
  between operations  0.64 us (1%)
    pallas_call x1, Pallas kernels, body(): pl.pallas_call(functools.partial(kernel, sizes), out_shape=(pltpu.VMEM((F...  47.6 us
    unnamed x2, local copies, waits for them, and re-layouts  1.18 us

profile of v4, /device:TPU:1, one launch (start us, length us, event | category | flops | bytes accessed | tf_op | source)
XLA Modules:
  0.0 49.5 jit_solution(10232201283830933159)
XLA Ops:
  0.6 47.6 %shard_map.104 = (f32[5,8,8,128]{3,2,1,0:T(8,128)S(1)}, f32[1,40]{1,0:T(1,128)S(1)}) custom-call(s32[8,8,16]{2,1,0:T(8,128)} %bitcast.2, s32[8,8,16]{2,1,0:T(8,128)} %bitcast.3, s32[1024]{0:T(1024)} %owner_hbm.1, f32[5,8,8,128]{3,2,1,0:T(8,128)} %adjoint_hbm.1, f32[8,8,128]{2,1,0:T(8,128)} %density_hbm.1, f32[3,8,8,128]{3,2,1,0:T(8,128)} %velocity_hbm.1, ...), custom_call_target="tpu_custom_call" | custom-call | tf_op jit(solution)/shard_map/pallas_call | solution.py:632
  48.3 0.7 %copy.13 = f32[5,8,8,128]{3,2,1,0:T(8,128)} copy(f32[5,8,8,128]{3,2,1,0:T(8,128)S(1)} %get-tuple-element.2) | data formatting | bytes 327680
  49.0 0.5 %copy.14 = f32[1,40]{1,0:T(1,128)} copy(f32[1,40]{1,0:T(1,128)S(1)} %get-tuple-element.3) | data formatting | bytes 320

commit v5 on v4

--- a/solution.py
+++ b/solution.py
@@ -16,6 +16,7 @@
 BOXES = Z // BZ
 TILE = 8
 ROWS = TILE // 2
+PARTS = 3
 LAYERS = 5
 STAGES = 3
 step_length = 0.14
@@ -62,7 +63,6 @@
     halo_layers,
     choose,
     row_choice,
-    spread,
     row_send,
     row_recv,
     cell_send,
@@ -360,8 +360,9 @@
                 owners[di, j, dk] = owner_of(i, j, jnp.clip(gz + dk, 0, n_gz - 1))
             return owners[di, j, dk]
 
-        lanes = lax.broadcasted_iota(jnp.int32, (1, n_row * ROWS), 1)
-        targets = [jnp.full((1, n_row * ROWS), -1, jnp.int32) for _ in range(2)]
+        shape = (1, PARTS * n_row * ROWS)
+        lanes = lax.rem(lax.broadcasted_iota(jnp.int32, shape, 1), n_row * ROWS)
+        targets = [jnp.full(shape, -1, jnp.int32) for _ in range(2)]
         for t in range(n_row):
             di, j = t // n_gy, t % n_gy
             bricks = [(0, di, j, 0, None)]
@@ -379,8 +380,9 @@
                     cell = jnp.where(there, cell, -1)
                 at = t * ROWS + r % ROWS
                 targets[r // ROWS] = jnp.where(lanes == at, cell, targets[r // ROWS])
-        cells = lax.broadcasted_iota(jnp.int32, (2 * n_plane * n_gz, n_row * ROWS), 0)
-        choose[...] = jnp.logical_or(cells == targets[0], cells == targets[1]).astype(jnp.float32)
+        cells = lax.broadcasted_iota(jnp.int32, choose.shape, 0)
+        chosen = jnp.logical_or(cells == targets[0], cells == targets[1])
+        choose[...] = jnp.where(chosen, 1.0, 0.0).astype(jnp.bfloat16)
         to_row = jnp.full((ROWS, Z), -1, jnp.int32)
         slots = packed_row + ROWS * packed_half
         places = [(me, None)]
@@ -392,11 +394,6 @@
                 row = jnp.where(there, row, -1)
             to_row = jnp.where(slots == r, row, to_row)
         row_choice[...] = to_row
-        spread_to = lax.broadcasted_iota(jnp.int32, (Z, Z), 1)
-        spread[...] = (
-            lax.broadcasted_iota(jnp.int32, (Z, Z), 0)
-            == BZ * lax.rem(spread_to, BOXES) + lax.div(spread_to, BOXES)
-        ).astype(jnp.float32)
 
     loads[5].wait()
     for side in range(2):
@@ -566,8 +563,12 @@
     for r in range(1, n_row):
         row_copy(r).wait_recv()
     rows = jnp.concatenate([row_recv[t] for t in range(n_row)], axis=0)
+    parts = []
+    for _ in range(PARTS):
+        parts.append(rows.astype(jnp.bfloat16))
+        rows = rows - parts[-1].astype(jnp.float32)
     cells = jnp.dot(
-        choose[...], rows, preferred_element_type=jnp.float32, precision=lax.Precision.HIGHEST
+        choose[...], jnp.concatenate(parts, axis=0), preferred_element_type=jnp.float32
     )
     n_cell = n_gz * n_plane
     first_half = lax.rem(lax.broadcasted_iota(jnp.int32, (n_cell, Z), 1), BZ) < BZ // 2
@@ -602,12 +603,22 @@
     for dz, dy in others:
         cell_copy(dz, dy).wait_recv()
     own = jnp.sum(cell_recv[...].reshape(n_gz * n_plane, Z), axis=0, keepdims=True)
-    ordered = jnp.dot(
-        own, spread[...], preferred_element_type=jnp.float32, precision=lax.Precision.HIGHEST
-    )
-    grad_ref[...] = ordered[:, : F * BOXES]
+    grad_ref[...] = own
     for dz, dy in others:
         cell_copy(dz, dy).wait_send()
+
+
+def write_out(fields, row, fields_out, gradient_out, gradient, sems):
+    copy = pltpu.make_async_copy(fields, fields_out, sems.at[0])
+    copy.start()
+    to = lax.broadcasted_iota(jnp.int32, (TILE, Z), 1)
+    place = BZ * lax.rem(to, BOXES) + lax.div(to, BOXES)
+    wide = jnp.broadcast_to(row[...], (TILE, Z))
+    gradient[...] = jnp.take_along_axis(wide, place, axis=1)[:1, : F * BOXES]
+    small = pltpu.make_async_copy(gradient, gradient_out, sems.at[1])
+    small.start()
+    copy.wait()
+    small.wait()
 
 
 def solution(mesh):
@@ -629,11 +640,11 @@
     ):
         f32 = jnp.float32
         hbm = pl.BlockSpec(memory_space=pl.ANY)
-        return pl.pallas_call(
+        fields, gradient = pl.pallas_call(
             functools.partial(kernel, sizes),
             out_shape=(
                 pltpu.VMEM((F, X, Y, Z), f32),
-                pltpu.VMEM((1, F * BOXES), f32),
+                pltpu.VMEM((1, Z), f32),
             ),
             in_specs=[hbm] * 9,
             out_specs=(pl.BlockSpec(memory_space=pltpu.VMEM),) * 2,
@@ -662,9 +673,8 @@
                 pltpu.VMEM((2, F, Y, Z), f32),
                 pltpu.VMEM((2, LAYERS, Y, Z), f32),
                 pltpu.VMEM((2, LAYERS, Y, Z), f32),
-                pltpu.VMEM((2 * n_plane * n_gz, n_row * ROWS), f32),
+                pltpu.VMEM((2 * n_plane * n_gz, PARTS * n_row * ROWS), jnp.bfloat16),
                 pltpu.VMEM((ROWS, Z), jnp.int32),
-                pltpu.VMEM((Z, Z), f32),
                 pltpu.VMEM((n_row, ROWS, Z), f32),
                 pltpu.VMEM((n_row, ROWS, Z), f32),
                 pltpu.VMEM((n_plane * n_gz, 1, Z), f32),
@@ -693,6 +703,19 @@
             sponge,
             source_shape,
         )
+        return pl.pallas_call(
+            write_out,
+            out_shape=(
+                jax.ShapeDtypeStruct((F, X, Y, Z), f32),
+                jax.ShapeDtypeStruct((1, F * BOXES), f32),
+            ),
+            in_specs=[pl.BlockSpec(memory_space=pltpu.VMEM)] * 2,
+            out_specs=(hbm, hbm),
+            scratch_shapes=[pltpu.VMEM((1, F * BOXES), f32), pltpu.SemaphoreType.DMA((2,))],
+        )(
+            pltpu.with_memory_space_constraint(fields, pltpu.VMEM),
+            pltpu.with_memory_space_constraint(gradient, pltpu.VMEM),
+        )
 
     in_specs = (
         P(None, "gx", "gy", "gz"),

time: 49.7 us -> 48.9 us (0.984)
  local copies, waits for them, and re-layouts: 1.18 us -> 0 us
  Pallas kernels: 47.6 us -> 48.1 us
    unnamed x2 -> x0, local copies, waits for them, and re-layouts: 1.18 us -> none
    pallas_call x0 -> x1, Pallas kernels: none -> 0.69 us  [body(): pl.pallas_call(write_out, out_shape=(jax.ShapeDtypeStruct((F, X, Y, Z), f...]
where the time goes in v5:
time: 48.9 us; the launch traced here: 48.7 us
  Pallas kernels  48.1 us (98%)
  between operations  0.64 us (1%)
    pallas_call x1, Pallas kernels, body(): pl.pallas_call(functools.partial(kernel, sizes), out_shape=(pltpu.VMEM((F...  47.4 us

profile of v5, /device:TPU:1, one launch (start us, length us, event | category | flops | bytes accessed | tf_op | source)
XLA Modules:
  0.0 48.7 jit_solution(865726863631981268)
XLA Ops:
  0.6 47.4 %shard_map.104 = (f32[5,8,8,128]{3,2,1,0:T(8,128)S(1)}, f32[1,128]{1,0:T(1,128)S(1)}) custom-call(s32[8,8,16]{2,1,0:T(8,128)} %bitcast.2, s32[8,8,16]{2,1,0:T(8,128)} %bitcast.3, s32[1024]{0:T(1024)} %owner_hbm.1, f32[5,8,8,128]{3,2,1,0:T(8,128)} %adjoint_hbm.1, f32[8,8,128]{2,1,0:T(8,128)} %density_hbm.1, f32[3,8,8,128]{3,2,1,0:T(8,128)} %velocity_hbm.1, ...), custom_call_target="tpu_custom_call" | custom-call | tf_op jit(solution)/shard_map/pallas_call | solution.py:643
  48.0 0.7 %shard_map.105 = (f32[5,8,8,128]{3,2,1,0:T(8,128)}, f32[1,40]{1,0:T(1,128)}) custom-call(f32[5,8,8,128]{3,2,1,0:T(8,128)S(1)} %get-tuple-element.4.fields, f32[1,128]{1,0:T(1,128)S(1)} %get-tuple-element.5.row), custom_call_target="tpu_custom_call" | custom-call | tf_op jit(solution)/shard_map/pallas_call | solution.py:706

commit v6 on v5

--- a/solution.py
+++ b/solution.py
@@ -415,30 +415,17 @@
         for x in range(X):
             v = [fields[k, f, x] for f in range(F)]
             joint = joint_term(v, x)
-            if 0 < x < X - 1:
-                q = flux(v, joint, x, 0)
-                for f in range(F):
-                    flux_x[k, x, f] = q[f]
             q = flux(v, joint, x, 2)
             columns = q + [source[x]] if k == 0 else q
             for f, column in enumerate(columns):
                 here = lane == f * X + x
                 packs[0] = jnp.where(here, jnp.broadcast_to(column[:, 0:1], (Y, Z)), packs[0])
                 packs[1] = jnp.where(here, jnp.broadcast_to(column[:, Z - 1 : Z], (Y, Z)), packs[1])
+            q = flux(v, joint, x, 1)
             for f in range(F):
-                fields[k + 1, f, x] = (
-                    damp[x] * v[f]
-                    + jnp.where(last_z, 0.0, pltpu.roll(q[f], Z - 1, 1))
-                    - jnp.where(first_z, 0.0, pltpu.roll(q[f], 1, 1))
-                )
-            q = flux(v, joint, x, 1)
+                flux_y[k, f, pl.ds(x * Y, Y), :] = q[f]
             if k == 0:
                 flux_y[k, F, pl.ds(x * Y, Y), :] = source[x]
-            for f in range(F):
-                flux_y[k, f, pl.ds(x * Y, Y), :] = q[f]
-                fields[k + 1, f, x] += jnp.where(last_y, 0.0, pltpu.roll(q[f], Y - 1, 0)) - jnp.where(
-                    first_y, 0.0, pltpu.roll(q[f], 1, 0)
-                )
         for side in range(2):
             send_z[k, side] = packs[side]
         send_halo(k, 2)
@@ -446,6 +433,24 @@
             for side in range(2):
                 send_y[k, side, f] = flux_y[k, f, pl.ds((Y - 1) * side, X, stride=Y), :]
         send_halo(k, 1)
+        for x in range(X):
+            v = [fields[k, f, x] for f in range(F)]
+            joint = joint_term(v, x)
+            if 0 < x < X - 1:
+                q = flux(v, joint, x, 0)
+                for f in range(F):
+                    flux_x[k, x, f] = q[f]
+            q = flux(v, joint, x, 2)
+            for f in range(F):
+                r = flux_y[k, f, pl.ds(x * Y, Y), :]
+                fields[k + 1, f, x] = (
+                    damp[x] * v[f]
+                    + jnp.where(last_z, 0.0, pltpu.roll(q[f], Z - 1, 1))
+                    - jnp.where(first_z, 0.0, pltpu.roll(q[f], 1, 1))
+                ) + (
+                    jnp.where(last_y, 0.0, pltpu.roll(r, Y - 1, 0))
+                    - jnp.where(first_y, 0.0, pltpu.roll(r, 1, 0))
+                )
         for x in range(X):
             for f in range(F):
                 if x == 0:

time: 48.9 us -> 48.9 us (level)
  no operation moved by 1% of the time
where the time goes in v6:
time: 48.9 us; the launch traced here: 48.7 us
  Pallas kernels  48 us (98%)
  between operations  0.64 us (1%)
    pallas_call x1, Pallas kernels, body(): pl.pallas_call(functools.partial(kernel, sizes), out_shape=(pltpu.VMEM((F...  47.3 us

profile of v6, /device:TPU:1, one launch (start us, length us, event | category | flops | bytes accessed | tf_op | source)
XLA Modules:
  0.0 48.7 jit_solution(6792347190360217071)
XLA Ops:
  0.6 47.3 %shard_map.104 = (f32[5,8,8,128]{3,2,1,0:T(8,128)S(1)}, f32[1,128]{1,0:T(1,128)S(1)}) custom-call(s32[8,8,16]{2,1,0:T(8,128)} %bitcast.2, s32[8,8,16]{2,1,0:T(8,128)} %bitcast.3, s32[1024]{0:T(1024)} %owner_hbm.1, f32[5,8,8,128]{3,2,1,0:T(8,128)} %adjoint_hbm.1, f32[8,8,128]{2,1,0:T(8,128)} %density_hbm.1, f32[3,8,8,128]{3,2,1,0:T(8,128)} %velocity_hbm.1, ...), custom_call_target="tpu_custom_call" | custom-call | tf_op jit(solution)/shard_map/pallas_call | solution.py:648
  48.0 0.7 %shard_map.105 = (f32[5,8,8,128]{3,2,1,0:T(8,128)}, f32[1,40]{1,0:T(1,128)}) custom-call(f32[5,8,8,128]{3,2,1,0:T(8,128)S(1)} %get-tuple-element.4.fields, f32[1,128]{1,0:T(1,128)S(1)} %get-tuple-element.5.row), custom_call_target="tpu_custom_call" | custom-call | tf_op jit(solution)/shard_map/pallas_call | solution.py:711
